TPU v7x, 32 devices: a whole 2x2x4 slice. The times are simulated.
32 devices in a mesh: section: 4 (over y, x), ctx: 8 (over z, core).
Axes of the slice: x: 2, y: 2, z: 4, core: 2. Of those that a mesh axis runs over, the one named last changes fastest.
Arguments:
- fwd_in: bfloat16 [4, 1152, 1024], P('section', 'ctx'), may hold values from -6 to 6
- bwd_saved: bfloat16 [4, 1152, 1024], P('section', 'ctx'), may hold values from -6 to 6
- bwd_cot: bfloat16 [4, 1152, 1024], P('section', 'ctx'), may hold values from -6 to 6
- new_tokens: bfloat16 [1024, 1024], P('ctx'), may hold values from -6 to 6
- loss_cot: bfloat16 [1024, 1024], P('ctx'), may hold values from -6 to 6
- gain: bfloat16 [4, 1024], P('section'), may hold values from 0.099609375 to 1.8984375
- w_query: bfloat16 [4, 1024, 1024], P('section'), may hold values from -2 to 2
- w_keyval: bfloat16 [4, 1024, 512], P('section'), may hold values from -2 to 2
- w_out: bfloat16 [4, 1024, 1024], P('section'), may hold values from -0.1875 to 0.1875
Outputs:
- fwd_next: bfloat16 [4, 1152, 1024], P('section', 'ctx')
- cot_next: bfloat16 [4, 1152, 1024], P('section', 'ctx')
All inputs are finite; a program needn't handle non-finite values.
Results may differ from a plain program's by a relative error of at most 0.012.
The roundings to bfloat16 on the way count: a program that leaves them out, or rounds other values in their place, can miss the bound.
Values may be sent and summed in bfloat16 or wider, within the bound.
A program may use at most 64 MiB of HBM per device.

v0:
```python
import functools

import jax
import jax.numpy as jnp
from jax import lax
from jax.experimental import pallas as pl
from jax.experimental.pallas import tpu as pltpu
from jax.sharding import PartitionSpec as P

HEADS = 16
KV_HEADS = 4
HEAD_DIM = 64
GROUP = 8
PAIR = 2
CHIPS = GROUP // PAIR
LOCAL = KV_HEADS // PAIR
SHARED = HEADS // KV_HEADS
LANES = 128
PIECES = 4
UNROLL = 3

epsilon = 1e-05
far = 1 << 30

bf16 = jnp.bfloat16
f32 = jnp.float32
NT = (((1,), (1,)), ((), ()))
NN = (((1,), (0,)), ((), ()))


def mul(a, b, dims=NN):
    return lax.dot_general(a, b, dims, preferred_element_type=f32)


def kernel(
    sections, mem,
    xf_h, xb_h, cot_h, gain_ref, wq_h, wkv_h, wo_h,
    outf_h, outb_h,
    xf, xb, cot, wq, wkv, wo, normed, kvf, kvb, kvt, qf, qb, gb, kpos,
    sd, ex, cat, acc, gsend, grecv, gpass, gsum, kvown, stacked, halves, gq_send, gq_all, mix_send, mix_all,
    of, ob,
    local_sem, pair_send, pair_recv, kv_send, kv_recv, gr_send, gr_recv, sec_send, sec_recv,
    hop_send, hop_recv,
):
    rows = xf_h.shape[0]
    width = xf_h.shape[1]
    both = PAIR * rows
    total = GROUP * rows
    stack = SHARED * both
    half = width // PAIR
    tokens = rows - mem

    ctx = lax.axis_index("ctx")
    section = lax.axis_index("section")
    member = lax.rem(ctx, GROUP)
    base = ctx - member
    core = lax.rem(member, PAIR)
    chip = member // PAIR
    other = 1 - core
    partner = base + chip * PAIR + other

    loads = []
    mine = pl.ds(core * rows, rows)
    for at, (src, dst) in enumerate(
        [
            (xb_h, xb.at[mine]), (wkv_h, wkv), (xf_h, xf.at[mine]),
            (wq_h, wq), (cot_h, cot.at[mine]), (wo_h, wo),
        ]
    ):
        copy = pltpu.make_async_copy(src, dst, local_sem.at[at])
        copy.start()
        loads.append(copy)
    load_xb, load_wkv, load_xf, load_wq, load_cot, load_wo = loads

    after = lax.rem(section + 1, sections)
    before = lax.rem(section + sections - 1, sections)
    barrier = pltpu.get_barrier_semaphore()
    for k in range(1, GROUP):
        pl.semaphore_signal(
            barrier, inc=1, device_id={"ctx": base + lax.rem(member + k, GROUP)},
            device_id_type=pl.DeviceIdType.MESH,
        )
    for neighbour in (after, before):
        pl.semaphore_signal(
            barrier, inc=1, device_id={"section": neighbour},
            device_id_type=pl.DeviceIdType.MESH,
        )
    pl.semaphore_wait(barrier, GROUP + 1)

    def remote(src, dst, send, recv, where):
        return pltpu.make_async_remote_copy(
            src_ref=src, dst_ref=dst, send_sem=send, recv_sem=recv,
            device_id=where, device_id_type=pl.DeviceIdType.MESH,
        )

    theirs = pl.ds(other * rows, rows)

    def pair_copy(at, src, dst):
        copy = remote(src, dst, pair_send.at[at], pair_recv.at[at], {"ctx": partner})
        copy.start()
        return copy

    pair_copies = [
        pair_copy(0, xb_h, xb.at[mine]),
        pair_copy(1, xf_h, xf.at[mine]),
        pair_copy(2, cot_h, cot.at[mine]),
    ]

    def pair_arrived(at, dst):
        remote(dst, dst, pair_send.at[at], pair_recv.at[at], {"ctx": partner}).wait_recv()

    for b in range(GROUP):
        inner = lax.broadcasted_iota(jnp.int32, (rows, LANES), 0)
        kpos[b * rows : (b + 1) * rows, :] = jnp.where(
            inner < mem, -1, b * tokens + inner - mem
        )

    gain = gain_ref[...].astype(f32)

    def norm(x):
        values = x.astype(f32)
        scale = lax.rsqrt(jnp.mean(values * values, axis=-1, keepdims=True) + epsilon)
        return values, scale

    def make_normed(x_ref, place):
        values, scale = norm(x_ref[place, :])
        normed[place, :] = (values * scale * gain).astype(bf16)

    last = CHIPS - 1
    is_end = jnp.logical_or(chip == 0, chip == last)
    is_middle = jnp.logical_not(is_end)
    opposite = last - chip
    hop_from = jnp.where(chip == 1, last, 0)
    hop_to = last - hop_from
    sum_via = jnp.where(chip == 0, 1, last - 1)
    sum_from = jnp.where(chip == 1, 0, last)

    def peer(k):
        return lax.rem(member + k, GROUP)

    def source(k):
        return lax.rem(member + GROUP - k, GROUP)

    def is_far(one):
        return jnp.logical_and(is_end, one // PAIR == opposite)

    order = sorted(range(1, GROUP), key=lambda k: abs(k - GROUP // 2))

    def project_kv(kv_ref, kind):
        keyval = mul(normed[mine, :], wkv[...])
        for h in range(KV_HEADS):
            at = h * HEAD_DIM
            after_keys = KV_HEADS * HEAD_DIM + at
            kvown[kind, h] = jnp.concatenate(
                [keyval[:, at : at + HEAD_DIM], keyval[:, after_keys : after_keys + HEAD_DIM]],
                axis=1,
            ).astype(bf16)
        for g in range(LOCAL):
            kv_ref[g, pl.ds(member * rows, rows), :] = kvown[kind, core * LOCAL + g]

    def kv_copy(kv_ref, kind, g, k):
        to = peer(k)
        return remote(
            kvown.at[kind, lax.rem(to, PAIR) * LOCAL + g],
            kv_ref.at[g, pl.ds(member * rows, rows)],
            kv_send.at[kind, g, k], kv_recv.at[kind, g, k], {"ctx": base + to},
        )

    def send_kv(kv_ref, kind):
        for g in range(LOCAL):
            for k in order:
                @pl.when(jnp.logical_not(is_far(peer(k))))
                def _():
                    kv_copy(kv_ref, kind, g, k).start()

    def finish_kv(kv_ref, kind):
        for g in range(LOCAL):
            for k in order:
                @pl.when(jnp.logical_not(is_far(peer(k))))
                def _():
                    kv_copy(kv_ref, kind, g, k).wait_send()

            @pl.when(is_middle)
            def _():
                hop_copy(kv_ref, kind, g).wait_send()

    def hop_copy(kv_ref, kind, g):
        place = kv_ref.at[g, pl.ds(hop_from * both, both)]
        return remote(
            place, place, hop_send.at[kind, g], hop_recv.at[kind, g],
            {"ctx": base + hop_to * PAIR + core},
        )

    def kv_wait(kv_ref, kind, g, one):
        k = lax.rem(member + GROUP - one, GROUP)
        place = kv_ref.at[g, pl.ds(one * rows, rows)]
        remote(
            place, place, kv_send.at[kind, g, k], kv_recv.at[kind, g, k], {"ctx": base + one}
        ).wait_recv()

    def hop_kv(kv_ref, kind, g):
        @pl.when(is_middle)
        def _():
            for c in range(PAIR):
                kv_wait(kv_ref, kind, g, hop_from * PAIR + c)
            hop_copy(kv_ref, kind, g).start()

    def kv_arrived(kv_ref, kind, g):
        for k in range(1, GROUP):
            one = source(k)
            done = jnp.logical_and(is_middle, one // PAIR == hop_from)

            @pl.when(jnp.logical_not(jnp.logical_or(is_far(one), done)))
            def _():
                kv_wait(kv_ref, kind, g, one)

        @pl.when(is_end)
        def _():
            place = kv_ref.at[g, pl.ds(opposite * both, both)]
            remote(
                place, place, hop_send.at[kind, g], hop_recv.at[kind, g],
                {"ctx": base + opposite * PAIR + core},
            ).wait_recv()

    def gr_copy(g, k):
        to = peer(k)
        return remote(
            gsend.at[g, pl.ds(to * rows, rows)], grecv.at[k, g],
            gr_send.at[g, k], gr_recv.at[g, k], {"ctx": base + to},
        )

    def is_summed(one):
        return jnp.logical_and(is_middle, one // PAIR == last - sum_from)

    def sum_copy(g, where):
        return remote(
            gsend.at[g, pl.ds(opposite * both, both)], gpass.at[g],
            hop_send.at[2, g], hop_recv.at[2, g], {"ctx": base + where * PAIR + core},
        )

    def send_sums(g):
        gsend[g] = acc[g].astype(bf16)

        @pl.when(is_end)
        def _():
            sum_copy(g, sum_via).start()

        for k in order:
            to = peer(k)

            @pl.when(jnp.logical_not(jnp.logical_or(is_far(to), is_summed(to))))
            def _():
                gr_copy(g, k).start()

    def hop_sums(g):
        @pl.when(is_middle)
        def _():
            sum_copy(g, sum_from).wait_recv()
            place = pl.ds((last - sum_from) * both, both)
            gsend[g, place, :] = (acc[g, place, :] + gpass[g].astype(f32)).astype(bf16)
            for k in order:
                @pl.when(is_summed(peer(k)))
                def _():
                    gr_copy(g, k).start()

    def finish_sums(g):
        @pl.when(is_end)
        def _():
            sum_copy(g, sum_via).wait_send()

        for k in order:
            @pl.when(jnp.logical_not(is_far(peer(k))))
            def _():
                gr_copy(g, k).wait_send()

    def spread(matrix, dst, upper, factor):
        rounded = matrix.astype(bf16).astype(f32) * factor
        zero = jnp.zeros((both, HEAD_DIM), f32)
        for g in range(LOCAL):
            for h in range(SHARED):
                at = (g * SHARED + h) * HEAD_DIM
                piece = rounded[:, at : at + HEAD_DIM]
                parts = [zero, piece] if upper else [piece, zero]
                dst[g, h * both : (h + 1) * both, :] = jnp.concatenate(parts, axis=1).astype(bf16)

    scale_by = HEAD_DIM ** (-0.5)
    my_cols = pl.ds(pl.multiple_of(core * half, half), half)

    load_xb.wait()
    make_normed(xb, mine)
    load_wkv.wait()
    project_kv(kvb, 0)
    send_kv(kvb, 0)
    pair_arrived(0, xb.at[theirs])
    make_normed(xb, theirs)
    load_wq.wait()
    spread(mul(normed[...], wq[:, my_cols]), qb, False, scale_by)
    load_cot.wait()
    pair_arrived(2, cot.at[theirs])
    load_wo.wait()
    spread(mul(cot[...], wo[my_cols, :], NT), gb, True, 1.0)
    load_xf.wait()
    make_normed(xf, mine)
    project_kv(kvf, 1)
    hop_kv(kvb, 0, 0)
    pair_arrived(1, xf.at[theirs])
    make_normed(xf, theirs)
    spread(mul(normed[...], wq[:, my_cols]), qf, False, scale_by)

    step = total // PIECES

    def query_positions(start):
        row = start + lax.broadcasted_iota(jnp.int32, (1, LANES), 1)
        for h in range(1, SHARED):
            row = jnp.where(row >= both, row - both, row)
        block = jnp.where(row >= rows, 1, 0)
        inner = row - block * rows
        return jnp.where(inner < mem, far, (chip * PAIR + block) * tokens + inner - mem)

    parts = [slice(p * step, (p + 1) * step) for p in range(PIECES)]

    def backward_chunk(g, chunks):
        starts = [pl.multiple_of(i * LANES, LANES) for i in chunks]
        pairs = [
            jnp.concatenate([qb[g, pl.ds(at, LANES), :], gb[g, pl.ds(at, LANES), :]], axis=0)
            for at in starts
        ]
        for u, start in enumerate(starts):
            position = query_positions(start)
            top = None
            for part in parts:
                product = mul(kvb[g, part, :], pairs[u], NT)
                scores = jnp.where(kpos[part, :] <= position, product[:, :LANES], -1e30)
                sd[u, part, :LANES] = scores
                sd[u, part, LANES:] = product[:, LANES:]
                peak = jnp.max(scores, axis=0, keepdims=True)
                top = peak if top is None else jnp.maximum(top, peak)
            norm_sum = jnp.zeros((1, LANES), f32)
            delta = jnp.zeros((1, LANES), f32)
            for part in parts:
                expd = jnp.exp(sd[u, part, :LANES] - top)
                ex[u, part, :] = expd
                norm_sum += jnp.sum(expd, axis=0, keepdims=True)
                delta += jnp.sum(expd * sd[u, part, LANES:], axis=0, keepdims=True)
            inverse = 1.0 / norm_sum
            delta = delta * inverse
            at = u * 2 * LANES
            for part in parts:
                probs = ex[u, part, :] * inverse
                cat[part, at + LANES : at + 2 * LANES] = probs.astype(bf16)
                cat[part, at : at + LANES] = (probs * (sd[u, part, LANES:] - delta)).astype(bf16)
        everything = jnp.concatenate(pairs, axis=0)
        for part in parts:
            acc[g, part, :] += mul(cat[part, :], everything)
        for u, start in enumerate(starts):
            at = u * 2 * LANES
            turned = mul(kvt[...], cat[:, at : at + LANES])
            stacked[g, pl.ds(start, LANES), :] = turned.T * scale_by

    def forward_chunk(g, chunks):
        for u, i in enumerate(chunks):
            start = pl.multiple_of(i * LANES, LANES)
            queries = qf[g, pl.ds(start, LANES), :]
            position = query_positions(start)
            top = None
            for part in parts:
                product = mul(kvf[g, part, :], queries, NT)
                scores = jnp.where(kpos[part, :] <= position, product, -1e30)
                sd[u, part, :LANES] = scores
                peak = jnp.max(scores, axis=0, keepdims=True)
                top = peak if top is None else jnp.maximum(top, peak)
            norm_sum = jnp.zeros((1, LANES), f32)
            for part in parts:
                expd = jnp.exp(sd[u, part, :LANES] - top)
                ex[u, part, :] = expd
                norm_sum += jnp.sum(expd, axis=0, keepdims=True)
            inverse = 1.0 / norm_sum
            for part in parts:
                cat[part, u * LANES : (u + 1) * LANES] = (ex[u, part, :] * inverse).astype(bf16)
        turned = mul(kvt[...], cat[:, : len(chunks) * LANES])
        for u, i in enumerate(chunks):
            start = pl.multiple_of(i * LANES, LANES)
            stacked[g, pl.ds(start, LANES), :] = turned[:, u * LANES : (u + 1) * LANES].T

    def gather_heads(upper):
        first = HEAD_DIM if upper else 0
        lanes = slice(first, first + HEAD_DIM)
        for g in range(LOCAL):
            for h in range(0, SHARED, 2):
                left = stacked[g, h * both : (h + 1) * both, lanes]
                right = stacked[g, (h + 1) * both : (h + 2) * both, lanes]
                at = (g * SHARED + h) * HEAD_DIM
                halves[:, at : at + LANES] = jnp.concatenate([left, right], axis=1).astype(bf16)

    def run(chunk, g, actions):
        def body(i, carry):
            for at, action in actions.items():
                pl.when(i == at)(action)
            chunk(g, [i * UNROLL + u for u in range(UNROLL)])
            return carry

        lax.fori_loop(0, stack // LANES // UNROLL, body, 0)

    def go_on():
        hop_kv(kvb, 0, 1)
        send_kv(kvf, 1)

    def late():
        hop_sums(0)
        hop_kv(kvf, 1, 1)

    backward_actions = [
        {1: go_on},
        {1: lambda: hop_kv(kvf, 1, 0), 2: late},
    ]
    for g in range(LOCAL):
        kv_arrived(kvb, 0, g)
        kvt[...] = kvb[g].astype(f32).T.astype(bf16)
        acc[g] = jnp.zeros((total, LANES), f32)
        run(backward_chunk, g, backward_actions[g])
        send_sums(g)
    gather_heads(False)
    gq_send[...] = halves[theirs, :]
    pair_copies.append(pair_copy(3, gq_send, gq_all.at[core]))
    gq_all[core] = halves[mine, :]

    for g in range(LOCAL):
        kv_arrived(kvf, 1, g)
        kvt[...] = kvf[g].astype(f32).T.astype(bf16)
        run(forward_chunk, g, {2: lambda: hop_sums(1)} if g == 0 else {})
    gather_heads(True)
    mix_send[...] = halves[theirs, :]
    pair_copies.append(pair_copy(4, mix_send, mix_all.at[core]))
    mix_all[core] = halves[mine, :]
    pair_arrived(4, mix_all.at[other])
    made = xf[mine, :].astype(f32)
    for p in range(PAIR):
        made += mul(mix_all[p], wo[p * half : (p + 1) * half, :])
    of[...] = made.astype(bf16)

    def shift(at, src, dst, where, edge, arrive_edge):
        small = remote(
            src.at[pl.ds(0, mem)], dst.at[pl.ds(0, mem)],
            sec_send.at[at, 0], sec_recv.at[at, 0], {"section": where},
        )
        large = remote(
            src.at[pl.ds(mem, tokens)], dst.at[pl.ds(mem, tokens)],
            sec_send.at[at, 1], sec_recv.at[at, 1], {"section": where},
        )
        small.start()

        @pl.when(section != edge)
        def _():
            large.start()

        def finish():
            small.wait()

            @pl.when(section != edge)
            def _():
                large.wait_send()

            @pl.when(section != arrive_edge)
            def _():
                large.wait_recv()

        return finish

    finish_f = shift(0, of, outf_h, after, sections - 1, 0)

    for g in range(LOCAL):
        own = acc[g, pl.ds(member * rows, rows), :]
        cross = None
        for k in range(1, GROUP):
            one = source(k)

            @pl.when(is_far(one))
            def _():
                grecv[k, g] = jnp.zeros((rows, LANES), bf16)

            @pl.when(jnp.logical_not(is_far(one)))
            def _():
                place = grecv.at[k, g]
                remote(
                    place, place, gr_send.at[g, k], gr_recv.at[g, k], {"ctx": base + one}
                ).wait_recv()

            value = grecv[k, g].astype(f32)
            if k % PAIR == 0:
                own = own + value
            else:
                cross = value if cross is None else cross + value
        gsum[core * LOCAL + g] = own
        gsum[other * LOCAL + g] = cross
    pair_arrived(3, gq_all.at[other])
    columns = [gsum[h, :, :HEAD_DIM] for h in range(KV_HEADS)]
    columns += [gsum[h, :, HEAD_DIM:] for h in range(KV_HEADS)]
    grad_kv = jnp.concatenate(columns, axis=1).astype(bf16)
    grad_normed = mul(grad_kv, wkv[...], NT)
    for p in range(PAIR):
        grad_normed += mul(gq_all[p], wq[:, p * half : (p + 1) * half], NT)
    values, scale = norm(xb[mine, :])
    plain = values * scale
    pushed = gain * grad_normed
    grad_in = cot[mine, :].astype(f32) + scale * (
        pushed - plain * jnp.mean(pushed * plain, axis=-1, keepdims=True)
    )
    ob[...] = grad_in.astype(bf16)
    finish_b = shift(1, ob, outb_h, before, 0, sections - 1)

    for copy in pair_copies:
        copy.wait_send()
    finish_kv(kvb, 0)
    finish_kv(kvf, 1)
    for g in range(LOCAL):
        finish_sums(g)
    finish_f()
    finish_b()


def shards(fwd_in, bwd_saved, bwd_cot, new_tokens, loss_cot, gain, w_query, w_keyval, w_out):
    section_now = lax.axis_index("section")
    sections = lax.axis_size("section")
    rows, width = fwd_in.shape[1:]
    mem = rows - new_tokens.shape[0]
    both = PAIR * rows
    total = GROUP * rows
    stack = SHARED * both
    half = width // PAIR
    anywhere = pl.BlockSpec(memory_space=pl.ANY)
    block = jax.ShapeDtypeStruct((rows, width), bf16)
    vmem = pltpu.VMEM
    dma = pltpu.SemaphoreType.DMA
    arrived, returned = pl.pallas_call(
        functools.partial(kernel, sections, mem),
        out_shape=(block, block),
        in_specs=[anywhere] * 3 + [pl.BlockSpec(memory_space=pltpu.VMEM)] + [anywhere] * 3,
        out_specs=(anywhere, anywhere),
        scratch_shapes=[
            vmem((both, width), bf16), vmem((both, width), bf16), vmem((both, width), bf16),
            vmem(w_query.shape[1:], bf16), vmem(w_keyval.shape[1:], bf16), vmem(w_out.shape[1:], bf16),
            vmem((both, width), bf16),
            vmem((LOCAL, total, LANES), bf16), vmem((LOCAL, total, LANES), bf16),
            vmem((LANES, total), bf16),
            vmem((LOCAL, stack, LANES), bf16), vmem((LOCAL, stack, LANES), bf16),
            vmem((LOCAL, stack, LANES), bf16),
            vmem((total, LANES), jnp.int32),
            vmem((UNROLL, total, 2 * LANES), f32), vmem((UNROLL, total, LANES), f32),
            vmem((total, UNROLL * 2 * LANES), bf16),
            vmem((LOCAL, total, LANES), f32), vmem((LOCAL, total, LANES), bf16),
            vmem((GROUP, LOCAL, rows, LANES), bf16), vmem((LOCAL, both, LANES), bf16),
            vmem((KV_HEADS, rows, LANES), f32), vmem((2, KV_HEADS, rows, LANES), bf16),
            vmem((LOCAL, stack, LANES), f32), vmem((both, half), bf16),
            vmem((rows, half), bf16), vmem((PAIR, rows, half), bf16),
            vmem((rows, half), bf16), vmem((PAIR, rows, half), bf16),
            vmem((rows, width), bf16), vmem((rows, width), bf16),
            dma((6,)), dma((5,)), dma((5,)),
            dma((2, LOCAL, GROUP)), dma((2, LOCAL, GROUP)),
            dma((LOCAL, GROUP)), dma((LOCAL, GROUP)),
            dma((2, 2)), dma((2, 2)),
            dma((3, LOCAL)), dma((3, LOCAL)),
        ],
        compiler_params=pltpu.CompilerParams(
            collective_id=0, has_side_effects=True, vmem_limit_bytes=60 * 1024 * 1024
        ),
    )(fwd_in[0], bwd_saved[0], bwd_cot[0], gain, w_query[0], w_keyval[0], w_out[0])
    token_row = lax.broadcasted_iota(jnp.int32, (rows, 1), 0) >= mem
    edge = jnp.pad(new_tokens, ((mem, 0), (0, 0)))
    fwd_next = jnp.where(token_row & (section_now == 0), edge, arrived)[None]
    edge = jnp.pad(loss_cot, ((mem, 0), (0, 0)))
    cot_next = jnp.where(token_row & (section_now == sections - 1), edge, returned)[None]
    return (fwd_next, cot_next)


def solution(mesh):
    return jax.shard_map(
        shards,
        mesh=mesh,
        in_specs=(
            P("section", "ctx", None),
            P("section", "ctx", None),
            P("section", "ctx", None),
            P("ctx", None),
            P("ctx", None),
            P("section", None),
            P("section", None, None),
            P("section", None, None),
            P("section", None, None),
        ),
        out_specs=(P("section", "ctx", None), P("section", "ctx", None)),
        check_vma=False,
    )
```

profile of v0, /device:TPU:1, one launch (start us, length us, event | category | flops | bytes accessed | tf_op | source)
XLA Modules:
  0.0 56.6 jit_solution(2137623879940189096)
XLA Ops:
  0.7 0.0 copy-start
  0.7 0.0 copy-start.1
  0.7 53.8 %shard_map.104 = (bf16[144,1024]{1,0:T(8,128)(2,1)}, bf16[144,1024]{1,0:T(8,128)(2,1)}) custom-call(bf16[144,1024]{1,0:T(8,128)(2,1)} %bitcast.13, bf16[144,1024]{1,0:T(8,128)(2,1)} %bitcast.14, bf16[144,1024]{1,0:T(8,128)(2,1)} %bitcast.15, bf16[1,1024]{1,0:T(2,128)(2,1)} %gain_ref.1, bf16[1024,1024]{1,0:T(8,128)(2,1)} %bitcast.10, ...), custom_call_target="tpu_custom_call" | custom-call | tf_op jit(solution)/shard_map/pallas_call | solution.py:534
  54.5 0.0 copy-done
  54.5 0.0 copy-done.1
  54.6 2.1 %select_bitcast_fusion = (bf16[1,144,1024]{2,1,0:T(8,128)(2,1)}, bf16[1,144,1024]{2,1,0:T(8,128)(2,1)}) fusion(bf16[144,1024]{1,0:T(8,128)(2,1)} %get-tuple-element.5, bf16[128,1024]{1,0:T(8,128)(2,1)S(1)} %copy-done, pred[144]{0:T(512)(128)(4,1)S(1)} %fusion, bf16[144,1024]{1,0:T(8,128)(2,1)} %get-tuple-element.4, bf16[128,1024]{1,0:T(8,128)(2,1)S(1)} %copy-done.1, ...), kind=kLoop, calls=%fused_computation | loop fusion | flops 294912 | bytes 1704224 | tf_op jit(solution)/shard_map/broadcast_in_dim | solution.py:571
  (2 shorter events, 0.0 us)
Async XLA Ops:
  0.7 53.9 %copy-start = (bf16[128,1024]{1,0:T(8,128)(2,1)S(1)}, bf16[128,1024]{1,0:T(8,128)(2,1)}, u32[]{:S(2)}) copy-start(bf16[128,1024]{1,0:T(8,128)(2,1)} %param.13) | copy-start | bytes 786436
  0.7 53.9 %copy-start.1 = (bf16[128,1024]{1,0:T(8,128)(2,1)S(1)}, bf16[128,1024]{1,0:T(8,128)(2,1)}, u32[]{:S(2)}) copy-start(bf16[128,1024]{1,0:T(8,128)(2,1)} %param.12) | copy-start | bytes 786436
where the time goes:
time: 56.8 us; the launch traced here: 56.6 us
  Pallas kernels  53.8 us (95%)
  other arithmetic  2.09 us (4%)
  between operations  0.69 us (1%)
    pallas_call x1, Pallas kernels, shards(): pl.pallas_call(functools.partial(kernel, sections, mem), out_shape=(block...  53.8 us
    broadcast_in_dim x1, other arithmetic, shards(): jnp.where(token_row & (section_now == sections - 1), edge, returned)[None]  2.07 us

commit v1 on v0

--- a/solution.py
+++ b/solution.py
@@ -34,11 +34,11 @@
 
 def kernel(
     sections, mem,
-    xf_h, xb_h, cot_h, gain_ref, wq_h, wkv_h, wo_h,
+    xf_h, xb_h, cot_h, gain_h, wq_h, wkv_h, wo_h,
     outf_h, outb_h,
-    xf, xb, cot, wq, wkv, wo, normed, kvf, kvb, kvt, qf, qb, gb, kpos,
-    sd, ex, cat, acc, gsend, grecv, gpass, gsum, kvown, stacked, halves, gq_send, gq_all, mix_send, mix_all,
-    of, ob,
+    xf, xb, cot, gain_v, wq, wkv, wo, normed, kvf, kvb, kvt, qf, qb, gb, kpos,
+    sd, ex, cat, acc, gsend, grecv, gpass, gsum, kvown, qx_send, qx_recv,
+    gq_my, gq_send, gq_recv, mix_my, mix_send, mix_recv, of, ob,
     local_sem, pair_send, pair_recv, kv_send, kv_recv, gr_send, gr_recv, sec_send, sec_recv,
     hop_send, hop_recv,
 ):
@@ -46,9 +46,12 @@
     width = xf_h.shape[1]
     both = PAIR * rows
     total = GROUP * rows
-    stack = SHARED * both
     half = width // PAIR
     tokens = rows - mem
+    slab = LANES // (PAIR * SHARED)
+    rounds = rows // slab // UNROLL
+    early = rounds - 1
+    cut = early * UNROLL * slab
 
     ctx = lax.axis_index("ctx")
     section = lax.axis_index("section")
@@ -59,19 +62,6 @@
     other = 1 - core
     partner = base + chip * PAIR + other
 
-    loads = []
-    mine = pl.ds(core * rows, rows)
-    for at, (src, dst) in enumerate(
-        [
-            (xb_h, xb.at[mine]), (wkv_h, wkv), (xf_h, xf.at[mine]),
-            (wq_h, wq), (cot_h, cot.at[mine]), (wo_h, wo),
-        ]
-    ):
-        copy = pltpu.make_async_copy(src, dst, local_sem.at[at])
-        copy.start()
-        loads.append(copy)
-    load_xb, load_wkv, load_xf, load_wq, load_cot, load_wo = loads
-
     after = lax.rem(section + 1, sections)
     before = lax.rem(section + sections - 1, sections)
     barrier = pltpu.get_barrier_semaphore()
@@ -85,7 +75,18 @@
             barrier, inc=1, device_id={"section": neighbour},
             device_id_type=pl.DeviceIdType.MESH,
         )
-    pl.semaphore_wait(barrier, GROUP + 1)
+
+    loads = []
+    for at, (src, dst) in enumerate(
+        [
+            (xb_h, xb), (gain_h, gain_v), (wkv_h, wkv), (wq_h, wq), (xf_h, xf),
+            (cot_h, cot), (wo_h, wo),
+        ]
+    ):
+        copy = pltpu.make_async_copy(src, dst, local_sem.at[at])
+        copy.start()
+        loads.append(copy)
+    load_xb, load_gain, load_wkv, load_wq, load_xf, load_cot, load_wo = loads
 
     def remote(src, dst, send, recv, where):
         return pltpu.make_async_remote_copy(
@@ -93,18 +94,12 @@
             device_id=where, device_id_type=pl.DeviceIdType.MESH,
         )
 
-    theirs = pl.ds(other * rows, rows)
+    pair_copies = []
 
     def pair_copy(at, src, dst):
         copy = remote(src, dst, pair_send.at[at], pair_recv.at[at], {"ctx": partner})
         copy.start()
-        return copy
-
-    pair_copies = [
-        pair_copy(0, xb_h, xb.at[mine]),
-        pair_copy(1, xf_h, xf.at[mine]),
-        pair_copy(2, cot_h, cot.at[mine]),
-    ]
+        pair_copies.append(copy)
 
     def pair_arrived(at, dst):
         remote(dst, dst, pair_send.at[at], pair_recv.at[at], {"ctx": partner}).wait_recv()
@@ -115,21 +110,20 @@
             inner < mem, -1, b * tokens + inner - mem
         )
 
-    gain = gain_ref[...].astype(f32)
-
     def norm(x):
         values = x.astype(f32)
         scale = lax.rsqrt(jnp.mean(values * values, axis=-1, keepdims=True) + epsilon)
         return values, scale
 
-    def make_normed(x_ref, place):
-        values, scale = norm(x_ref[place, :])
-        normed[place, :] = (values * scale * gain).astype(bf16)
+    def make_normed(x_ref):
+        values, scale = norm(x_ref[...])
+        normed[...] = (values * scale * gain_v[...].astype(f32)).astype(bf16)
 
     last = CHIPS - 1
     is_end = jnp.logical_or(chip == 0, chip == last)
     is_middle = jnp.logical_not(is_end)
     opposite = last - chip
+    adjacent = jnp.where(chip == 0, 1, last - 1)
     hop_from = jnp.where(chip == 1, last, 0)
     hop_to = last - hop_from
     sum_via = jnp.where(chip == 0, 1, last - 1)
@@ -147,7 +141,7 @@
     order = sorted(range(1, GROUP), key=lambda k: abs(k - GROUP // 2))
 
     def project_kv(kv_ref, kind):
-        keyval = mul(normed[mine, :], wkv[...])
+        keyval = mul(normed[...], wkv[...])
         for h in range(KV_HEADS):
             at = h * HEAD_DIM
             after_keys = KV_HEADS * HEAD_DIM + at
@@ -166,12 +160,11 @@
             kv_send.at[kind, g, k], kv_recv.at[kind, g, k], {"ctx": base + to},
         )
 
-    def send_kv(kv_ref, kind):
-        for g in range(LOCAL):
-            for k in order:
-                @pl.when(jnp.logical_not(is_far(peer(k))))
-                def _():
-                    kv_copy(kv_ref, kind, g, k).start()
+    def send_kv(kv_ref, kind, g):
+        for k in order:
+            @pl.when(jnp.logical_not(is_far(peer(k))))
+            def _():
+                kv_copy(kv_ref, kind, g, k).start()
 
     def finish_kv(kv_ref, kind):
         for g in range(LOCAL):
@@ -205,10 +198,18 @@
                 kv_wait(kv_ref, kind, g, hop_from * PAIR + c)
             hop_copy(kv_ref, kind, g).start()
 
-    def kv_arrived(kv_ref, kind, g):
+    def near_kv(kv_ref, kind, g):
+        @pl.when(is_end)
+        def _():
+            for c in range(PAIR):
+                kv_wait(kv_ref, kind, g, adjacent * PAIR + c)
+
+    def kv_arrived(kv_ref, kind, g, near_done=False):
         for k in range(1, GROUP):
             one = source(k)
             done = jnp.logical_and(is_middle, one // PAIR == hop_from)
+            if near_done:
+                done = jnp.logical_or(done, jnp.logical_and(is_end, one // PAIR == adjacent))
 
             @pl.when(jnp.logical_not(jnp.logical_or(is_far(one), done)))
             def _():
@@ -273,51 +274,77 @@
             def _():
                 gr_copy(g, k).wait_send()
 
-    def spread(matrix, dst, upper, factor):
-        rounded = matrix.astype(bf16).astype(f32) * factor
-        zero = jnp.zeros((both, HEAD_DIM), f32)
+    def spread(matrix, dst, block, upper, factor):
+        rounded = matrix.astype(f32) * factor
+        zero = jnp.zeros((rows, HEAD_DIM), f32)
         for g in range(LOCAL):
             for h in range(SHARED):
                 at = (g * SHARED + h) * HEAD_DIM
                 piece = rounded[:, at : at + HEAD_DIM]
                 parts = [zero, piece] if upper else [piece, zero]
-                dst[g, h * both : (h + 1) * both, :] = jnp.concatenate(parts, axis=1).astype(bf16)
+                wide = jnp.concatenate(parts, axis=1).astype(bf16)
+                for i in range(rows // slab):
+                    to = i * LANES + (block * SHARED + h) * slab
+                    dst[g, to : to + slab, :] = wide[i * slab : (i + 1) * slab, :]
 
     scale_by = HEAD_DIM ** (-0.5)
     my_cols = pl.ds(pl.multiple_of(core * half, half), half)
+    their_cols = pl.ds(pl.multiple_of(other * half, half), half)
+
+    def make_query(at, q_ref):
+        qx_send[at] = mul(normed[...], wq[:, their_cols]).astype(bf16)
+        spread(mul(normed[...], wq[:, my_cols]).astype(bf16), q_ref, 0, False, scale_by)
 
     load_xb.wait()
-    make_normed(xb, mine)
+    load_gain.wait()
+    make_normed(xb)
     load_wkv.wait()
     project_kv(kvb, 0)
-    send_kv(kvb, 0)
-    pair_arrived(0, xb.at[theirs])
-    make_normed(xb, theirs)
     load_wq.wait()
-    spread(mul(normed[...], wq[:, my_cols]), qb, False, scale_by)
+    make_query(0, qb)
+    load_xf.wait()
+    make_normed(xf)
+    project_kv(kvf, 1)
+    pl.semaphore_wait(barrier, GROUP + 1)
+    send_kv(kvb, 0, 0)
+    pair_copy(0, qx_send.at[0], qx_recv.at[0])
     load_cot.wait()
-    pair_arrived(2, cot.at[theirs])
     load_wo.wait()
-    spread(mul(cot[...], wo[my_cols, :], NT), gb, True, 1.0)
-    load_xf.wait()
-    make_normed(xf, mine)
-    project_kv(kvf, 1)
+    qx_send[2] = mul(cot[...], wo[their_cols, :], NT).astype(bf16)
+    pair_copy(2, qx_send.at[2], qx_recv.at[2])
+    spread(mul(cot[...], wo[my_cols, :], NT).astype(bf16), gb, 0, True, 1.0)
+    make_query(1, qf)
+    pair_copy(1, qx_send.at[1], qx_recv.at[1])
+    pair_arrived(0, qx_recv.at[0])
+    spread(qx_recv[0], qb, 1, False, scale_by)
+    pair_arrived(2, qx_recv.at[2])
+    spread(qx_recv[2], gb, 1, True, 1.0)
+    near_kv(kvb, 0, 0)
     hop_kv(kvb, 0, 0)
-    pair_arrived(1, xf.at[theirs])
-    make_normed(xf, theirs)
-    spread(mul(normed[...], wq[:, my_cols]), qf, False, scale_by)
+    send_kv(kvb, 0, 1)
+    pair_arrived(1, qx_recv.at[1])
+    spread(qx_recv[1], qf, 1, False, scale_by)
 
     step = total // PIECES
 
-    def query_positions(start):
-        row = start + lax.broadcasted_iota(jnp.int32, (1, LANES), 1)
-        for h in range(1, SHARED):
-            row = jnp.where(row >= both, row - both, row)
-        block = jnp.where(row >= rows, 1, 0)
-        inner = row - block * rows
-        return jnp.where(inner < mem, far, (chip * PAIR + block) * tokens + inner - mem)
+    def query_positions(i):
+        lane = lax.broadcasted_iota(jnp.int32, (1, LANES), 1)
+        block = jnp.where(lane < LANES // PAIR, member, chip * PAIR + other)
+        inner = i * slab + lax.rem(lane, slab)
+        return jnp.where(inner < mem, far, block * tokens + inner - mem)
 
     parts = [slice(p * step, (p + 1) * step) for p in range(PIECES)]
+
+    def put_heads(g, i, turned, mine_ref, theirs_ref):
+        place = pl.ds(pl.multiple_of(i * slab, slab), slab)
+        for block, ref in enumerate((mine_ref, theirs_ref)):
+            for h in range(0, SHARED, 2):
+                at = (block * SHARED + h) * slab
+                pair = jnp.concatenate(
+                    [turned[at : at + slab, :], turned[at + slab : at + 2 * slab, :]], axis=1
+                )
+                to = (g * SHARED + h) * HEAD_DIM
+                ref[place, to : to + LANES] = pair.astype(bf16)
 
     def backward_chunk(g, chunks):
         starts = [pl.multiple_of(i * LANES, LANES) for i in chunks]
@@ -325,8 +352,8 @@
             jnp.concatenate([qb[g, pl.ds(at, LANES), :], gb[g, pl.ds(at, LANES), :]], axis=0)
             for at in starts
         ]
-        for u, start in enumerate(starts):
-            position = query_positions(start)
+        for u, i in enumerate(chunks):
+            position = query_positions(i)
             top = None
             for part in parts:
                 product = mul(kvb[g, part, :], pairs[u], NT)
@@ -352,16 +379,16 @@
         everything = jnp.concatenate(pairs, axis=0)
         for part in parts:
             acc[g, part, :] += mul(cat[part, :], everything)
-        for u, start in enumerate(starts):
+        for u, i in enumerate(chunks):
             at = u * 2 * LANES
-            turned = mul(kvt[...], cat[:, at : at + LANES])
-            stacked[g, pl.ds(start, LANES), :] = turned.T * scale_by
+            turned = mul(kvt[:HEAD_DIM, :], cat[:, at : at + LANES])
+            put_heads(g, i, turned.T * scale_by, gq_my, gq_send)
 
     def forward_chunk(g, chunks):
         for u, i in enumerate(chunks):
             start = pl.multiple_of(i * LANES, LANES)
             queries = qf[g, pl.ds(start, LANES), :]
-            position = query_positions(start)
+            position = query_positions(i)
             top = None
             for part in parts:
                 product = mul(kvf[g, part, :], queries, NT)
@@ -377,84 +404,62 @@
             inverse = 1.0 / norm_sum
             for part in parts:
                 cat[part, u * LANES : (u + 1) * LANES] = (ex[u, part, :] * inverse).astype(bf16)
-        turned = mul(kvt[...], cat[:, : len(chunks) * LANES])
+        turned = mul(kvt[HEAD_DIM:, :], cat[:, : len(chunks) * LANES])
         for u, i in enumerate(chunks):
-            start = pl.multiple_of(i * LANES, LANES)
-            stacked[g, pl.ds(start, LANES), :] = turned[:, u * LANES : (u + 1) * LANES].T
-
-    def gather_heads(upper):
-        first = HEAD_DIM if upper else 0
-        lanes = slice(first, first + HEAD_DIM)
-        for g in range(LOCAL):
-            for h in range(0, SHARED, 2):
-                left = stacked[g, h * both : (h + 1) * both, lanes]
-                right = stacked[g, (h + 1) * both : (h + 2) * both, lanes]
-                at = (g * SHARED + h) * HEAD_DIM
-                halves[:, at : at + LANES] = jnp.concatenate([left, right], axis=1).astype(bf16)
-
-    def run(chunk, g, actions):
+            put_heads(g, i, turned[:, u * LANES : (u + 1) * LANES].T, mix_my, mix_send)
+
+    def run(chunk, g, begin, end, actions):
         def body(i, carry):
             for at, action in actions.items():
                 pl.when(i == at)(action)
             chunk(g, [i * UNROLL + u for u in range(UNROLL)])
             return carry
 
-        lax.fori_loop(0, stack // LANES // UNROLL, body, 0)
-
-    def go_on():
+        lax.fori_loop(begin, end, body, 0)
+
+    def turn(kv_ref, g):
+        kvt[...] = kv_ref[g].astype(f32).T.astype(bf16)
+
+    def after_first():
         hop_kv(kvb, 0, 1)
-        send_kv(kvf, 1)
-
-    def late():
-        hop_sums(0)
-        hop_kv(kvf, 1, 1)
+        send_kv(kvf, 1, 0)
+
+    def after_sums():
+        hop_kv(kvf, 1, 0)
+        send_kv(kvf, 1, 1)
 
     backward_actions = [
-        {1: go_on},
-        {1: lambda: hop_kv(kvf, 1, 0), 2: late},
+        {1: after_first},
+        {0: after_sums, 1: lambda: hop_sums(0), 2: lambda: hop_kv(kvf, 1, 1)},
     ]
     for g in range(LOCAL):
-        kv_arrived(kvb, 0, g)
-        kvt[...] = kvb[g].astype(f32).T.astype(bf16)
+        kv_arrived(kvb, 0, g, g == 0)
+        turn(kvb, g)
         acc[g] = jnp.zeros((total, LANES), f32)
-        run(backward_chunk, g, backward_actions[g])
+        run(backward_chunk, g, 0, rounds, backward_actions[g])
         send_sums(g)
-    gather_heads(False)
-    gq_send[...] = halves[theirs, :]
-    pair_copies.append(pair_copy(3, gq_send, gq_all.at[core]))
-    gq_all[core] = halves[mine, :]
-
-    for g in range(LOCAL):
-        kv_arrived(kvf, 1, g)
-        kvt[...] = kvf[g].astype(f32).T.astype(bf16)
-        run(forward_chunk, g, {2: lambda: hop_sums(1)} if g == 0 else {})
-    gather_heads(True)
-    mix_send[...] = halves[theirs, :]
-    pair_copies.append(pair_copy(4, mix_send, mix_all.at[core]))
-    mix_all[core] = halves[mine, :]
-    pair_arrived(4, mix_all.at[other])
-    made = xf[mine, :].astype(f32)
-    for p in range(PAIR):
-        made += mul(mix_all[p], wo[p * half : (p + 1) * half, :])
-    of[...] = made.astype(bf16)
-
-    def shift(at, src, dst, where, edge, arrive_edge):
-        small = remote(
-            src.at[pl.ds(0, mem)], dst.at[pl.ds(0, mem)],
-            sec_send.at[at, 0], sec_recv.at[at, 0], {"section": where},
-        )
-        large = remote(
-            src.at[pl.ds(mem, tokens)], dst.at[pl.ds(mem, tokens)],
-            sec_send.at[at, 1], sec_recv.at[at, 1], {"section": where},
-        )
-        small.start()
+    pair_copy(3, gq_send, gq_recv)
+
+    def shift(at, src, dst, where, begin, end, edge, arrive_edge):
+        def copy(index, first, stop):
+            place = pl.ds(first, stop - first)
+            return remote(
+                src.at[place], dst.at[place],
+                sec_send.at[at, index], sec_recv.at[at, index], {"section": where},
+            )
+
+        small = copy(0, begin, mem) if begin < mem else None
+        large = copy(1, max(begin, mem), end)
+        if small is not None:
+            small.start()
 
         @pl.when(section != edge)
         def _():
             large.start()
 
         def finish():
-            small.wait()
+            if small is not None:
+                small.wait()
 
             @pl.when(section != edge)
             def _():
@@ -466,7 +471,22 @@
 
         return finish
 
-    finish_f = shift(0, of, outf_h, after, sections - 1, 0)
+    def project_out(at, begin, end):
+        place = slice(begin, end)
+        pair_copy(4 + at, mix_send.at[place], mix_recv.at[place])
+        made = xf[place, :].astype(f32) + mul(mix_my[place, :], wo[my_cols, :])
+        pair_arrived(4 + at, mix_recv.at[place])
+        made += mul(mix_recv[place, :], wo[their_cols, :])
+        of[place, :] = made.astype(bf16)
+        return shift(at, of, outf_h, after, begin, end, sections - 1, 0)
+
+    for g in range(LOCAL):
+        if g == 1:
+            hop_sums(1)
+        kv_arrived(kvf, 1, g)
+        turn(kvf, g)
+        run(forward_chunk, g, 0, early, {})
+    finish_early = project_out(0, 0, cut)
 
     for g in range(LOCAL):
         own = acc[g, pl.ds(member * rows, rows), :]
@@ -492,21 +512,26 @@
                 cross = value if cross is None else cross + value
         gsum[core * LOCAL + g] = own
         gsum[other * LOCAL + g] = cross
-    pair_arrived(3, gq_all.at[other])
+    pair_arrived(3, gq_recv)
     columns = [gsum[h, :, :HEAD_DIM] for h in range(KV_HEADS)]
     columns += [gsum[h, :, HEAD_DIM:] for h in range(KV_HEADS)]
     grad_kv = jnp.concatenate(columns, axis=1).astype(bf16)
     grad_normed = mul(grad_kv, wkv[...], NT)
-    for p in range(PAIR):
-        grad_normed += mul(gq_all[p], wq[:, p * half : (p + 1) * half], NT)
-    values, scale = norm(xb[mine, :])
+    grad_normed += mul(gq_my[...], wq[:, my_cols], NT)
+    grad_normed += mul(gq_recv[...], wq[:, their_cols], NT)
+    values, scale = norm(xb[...])
     plain = values * scale
-    pushed = gain * grad_normed
-    grad_in = cot[mine, :].astype(f32) + scale * (
+    pushed = gain_v[...].astype(f32) * grad_normed
+    grad_in = cot[...].astype(f32) + scale * (
         pushed - plain * jnp.mean(pushed * plain, axis=-1, keepdims=True)
     )
     ob[...] = grad_in.astype(bf16)
-    finish_b = shift(1, ob, outb_h, before, 0, sections - 1)
+    finish_b = shift(2, ob, outb_h, before, 0, rows, 0, sections - 1)
+
+    for g in range(LOCAL):
+        turn(kvf, g)
+        run(forward_chunk, g, early, rounds, {})
+    finish_late = project_out(1, cut, rows)
 
     for copy in pair_copies:
         copy.wait_send()
@@ -514,7 +539,8 @@
     finish_kv(kvf, 1)
     for g in range(LOCAL):
         finish_sums(g)
-    finish_f()
+    finish_early()
+    finish_late()
     finish_b()
 
 
@@ -528,18 +554,20 @@
     stack = SHARED * both
     half = width // PAIR
     anywhere = pl.BlockSpec(memory_space=pl.ANY)
+    far_memory = pl.BlockSpec(memory_space=pltpu.HBM)
     block = jax.ShapeDtypeStruct((rows, width), bf16)
     vmem = pltpu.VMEM
     dma = pltpu.SemaphoreType.DMA
     arrived, returned = pl.pallas_call(
         functools.partial(kernel, sections, mem),
         out_shape=(block, block),
-        in_specs=[anywhere] * 3 + [pl.BlockSpec(memory_space=pltpu.VMEM)] + [anywhere] * 3,
+        in_specs=[far_memory] * 7,
         out_specs=(anywhere, anywhere),
         scratch_shapes=[
-            vmem((both, width), bf16), vmem((both, width), bf16), vmem((both, width), bf16),
+            vmem((rows, width), bf16), vmem((rows, width), bf16), vmem((rows, width), bf16),
+            vmem((1, width), bf16),
             vmem(w_query.shape[1:], bf16), vmem(w_keyval.shape[1:], bf16), vmem(w_out.shape[1:], bf16),
-            vmem((both, width), bf16),
+            vmem((rows, width), bf16),
             vmem((LOCAL, total, LANES), bf16), vmem((LOCAL, total, LANES), bf16),
             vmem((LANES, total), bf16),
             vmem((LOCAL, stack, LANES), bf16), vmem((LOCAL, stack, LANES), bf16),
@@ -550,18 +578,18 @@
             vmem((LOCAL, total, LANES), f32), vmem((LOCAL, total, LANES), bf16),
             vmem((GROUP, LOCAL, rows, LANES), bf16), vmem((LOCAL, both, LANES), bf16),
             vmem((KV_HEADS, rows, LANES), f32), vmem((2, KV_HEADS, rows, LANES), bf16),
-            vmem((LOCAL, stack, LANES), f32), vmem((both, half), bf16),
-            vmem((rows, half), bf16), vmem((PAIR, rows, half), bf16),
-            vmem((rows, half), bf16), vmem((PAIR, rows, half), bf16),
+            vmem((3, rows, half), bf16), vmem((3, rows, half), bf16),
+            vmem((rows, half), bf16), vmem((rows, half), bf16), vmem((rows, half), bf16),
+            vmem((rows, half), bf16), vmem((rows, half), bf16), vmem((rows, half), bf16),
             vmem((rows, width), bf16), vmem((rows, width), bf16),
-            dma((6,)), dma((5,)), dma((5,)),
+            dma((7,)), dma((6,)), dma((6,)),
             dma((2, LOCAL, GROUP)), dma((2, LOCAL, GROUP)),
             dma((LOCAL, GROUP)), dma((LOCAL, GROUP)),
-            dma((2, 2)), dma((2, 2)),
+            dma((3, 2)), dma((3, 2)),
             dma((3, LOCAL)), dma((3, LOCAL)),
         ],
         compiler_params=pltpu.CompilerParams(
-            collective_id=0, has_side_effects=True, vmem_limit_bytes=60 * 1024 * 1024
+            collective_id=0, has_side_effects=True, vmem_limit_bytes=60500 * 1024
         ),
     )(fwd_in[0], bwd_saved[0], bwd_cot[0], gain, w_query[0], w_keyval[0], w_out[0])
     token_row = lax.broadcasted_iota(jnp.int32, (rows, 1), 0) >= mem

time: 56.8 us -> 56.2 us (0.989)
  the two profiles are of different devices: /device:TPU:1 before, /device:TPU:5 now
where the time goes in v1:
time: 56.2 us; the launch traced here: 55.7 us
  Pallas kernels  52.9 us (94%)
  other arithmetic  2.09 us (4%)
  between operations  0.69 us (1%)
    pallas_call x1, Pallas kernels, shards(): pl.pallas_call(functools.partial(kernel, sections, mem), out_shape=(block...  52.9 us
    broadcast_in_dim x1, other arithmetic, shards(): jnp.where(token_row & (section_now == sections - 1), edge, returned)[None]  2.07 us

profile of v1, /device:TPU:5, one launch (start us, length us, event | category | flops | bytes accessed | tf_op | source)
XLA Modules:
  0.0 55.7 jit_solution(17959854133646268603)
XLA Ops:
  0.7 0.0 copy-start
  0.7 0.0 copy-start.1
  0.7 52.9 %shard_map.104 = (bf16[144,1024]{1,0:T(8,128)(2,1)}, bf16[144,1024]{1,0:T(8,128)(2,1)}) custom-call(bf16[144,1024]{1,0:T(8,128)(2,1)} %bitcast.13, bf16[144,1024]{1,0:T(8,128)(2,1)} %bitcast.14, bf16[144,1024]{1,0:T(8,128)(2,1)} %bitcast.15, bf16[1,1024]{1,0:T(2,128)(2,1)} %gain_h.1, bf16[1024,1024]{1,0:T(8,128)(2,1)} %bitcast.10, ...), custom_call_target="tpu_custom_call" | custom-call | tf_op jit(solution)/shard_map/pallas_call | solution.py:561
  53.6 0.0 copy-done
  53.6 0.0 copy-done.1
  53.6 2.1 %select_bitcast_fusion = (bf16[1,144,1024]{2,1,0:T(8,128)(2,1)}, bf16[1,144,1024]{2,1,0:T(8,128)(2,1)}) fusion(bf16[144,1024]{1,0:T(8,128)(2,1)} %get-tuple-element.5, bf16[128,1024]{1,0:T(8,128)(2,1)S(1)} %copy-done, pred[144]{0:T(512)(128)(4,1)S(1)} %fusion, bf16[144,1024]{1,0:T(8,128)(2,1)} %get-tuple-element.4, bf16[128,1024]{1,0:T(8,128)(2,1)S(1)} %copy-done.1, ...), kind=kLoop, calls=%fused_computation | loop fusion | flops 294912 | bytes 1704224 | tf_op jit(solution)/shard_map/broadcast_in_dim | solution.py:599
  (2 shorter events, 0.0 us)
Async XLA Ops:
  0.7 52.9 %copy-start = (bf16[128,1024]{1,0:T(8,128)(2,1)S(1)}, bf16[128,1024]{1,0:T(8,128)(2,1)}, u32[]{:S(2)}) copy-start(bf16[128,1024]{1,0:T(8,128)(2,1)} %param.13) | copy-start | bytes 786436
  0.7 52.9 %copy-start.1 = (bf16[128,1024]{1,0:T(8,128)(2,1)S(1)}, bf16[128,1024]{1,0:T(8,128)(2,1)}, u32[]{:S(2)}) copy-start(bf16[128,1024]{1,0:T(8,128)(2,1)} %param.12) | copy-start | bytes 786436

commit v2 on v1

--- a/solution.py
+++ b/solution.py
@@ -50,8 +50,6 @@
     tokens = rows - mem
     slab = LANES // (PAIR * SHARED)
     rounds = rows // slab // UNROLL
-    early = rounds - 1
-    cut = early * UNROLL * slab
 
     ctx = lax.axis_index("ctx")
     section = lax.axis_index("section")
@@ -123,7 +121,9 @@
     is_end = jnp.logical_or(chip == 0, chip == last)
     is_middle = jnp.logical_not(is_end)
     opposite = last - chip
-    adjacent = jnp.where(chip == 0, 1, last - 1)
+    nearest_end = jnp.where(chip == 1, 0, last)
+    adjacent = jnp.where(is_end, jnp.where(chip == 0, 1, last - 1), nearest_end)
+    hop_at = jnp.where(chip == 0, last - 1, 1)
     hop_from = jnp.where(chip == 1, last, 0)
     hop_to = last - hop_from
     sum_via = jnp.where(chip == 0, 1, last - 1)
@@ -160,9 +160,19 @@
             kv_send.at[kind, g, k], kv_recv.at[kind, g, k], {"ctx": base + to},
         )
 
-    def send_kv(kv_ref, kind, g):
+    def is_first(one):
+        away = one // PAIR
+        ends = jnp.logical_and(is_end, jnp.logical_or(away == hop_at, away == chip))
+        return jnp.logical_or(ends, jnp.logical_and(is_middle, away == adjacent))
+
+    def send_kv(kv_ref, kind, g, phase=None):
         for k in order:
-            @pl.when(jnp.logical_not(is_far(peer(k))))
+            use = jnp.logical_not(is_far(peer(k)))
+            if phase is not None:
+                first = is_first(peer(k))
+                use = jnp.logical_and(use, first if phase == 0 else jnp.logical_not(first))
+
+            @pl.when(use)
             def _():
                 kv_copy(kv_ref, kind, g, k).start()
 
@@ -300,21 +310,20 @@
     make_normed(xb)
     load_wkv.wait()
     project_kv(kvb, 0)
+    pl.semaphore_wait(barrier, GROUP + 1)
+    send_kv(kvb, 0, 0, 0)
     load_wq.wait()
     make_query(0, qb)
-    load_xf.wait()
-    make_normed(xf)
-    project_kv(kvf, 1)
-    pl.semaphore_wait(barrier, GROUP + 1)
-    send_kv(kvb, 0, 0)
+    send_kv(kvb, 0, 0, 1)
     pair_copy(0, qx_send.at[0], qx_recv.at[0])
     load_cot.wait()
     load_wo.wait()
     qx_send[2] = mul(cot[...], wo[their_cols, :], NT).astype(bf16)
     pair_copy(2, qx_send.at[2], qx_recv.at[2])
     spread(mul(cot[...], wo[my_cols, :], NT).astype(bf16), gb, 0, True, 1.0)
-    make_query(1, qf)
-    pair_copy(1, qx_send.at[1], qx_recv.at[1])
+    load_xf.wait()
+    make_normed(xf)
+    project_kv(kvf, 1)
     pair_arrived(0, qx_recv.at[0])
     spread(qx_recv[0], qb, 1, False, scale_by)
     pair_arrived(2, qx_recv.at[2])
@@ -322,8 +331,8 @@
     near_kv(kvb, 0, 0)
     hop_kv(kvb, 0, 0)
     send_kv(kvb, 0, 1)
-    pair_arrived(1, qx_recv.at[1])
-    spread(qx_recv[1], qf, 1, False, scale_by)
+    make_query(1, qf)
+    pair_copy(1, qx_send.at[1], qx_recv.at[1])
 
     step = total // PIECES
 
@@ -343,8 +352,8 @@
                 pair = jnp.concatenate(
                     [turned[at : at + slab, :], turned[at + slab : at + 2 * slab, :]], axis=1
                 )
-                to = (g * SHARED + h) * HEAD_DIM
-                ref[place, to : to + LANES] = pair.astype(bf16)
+                to = pl.multiple_of((g * SHARED + h) * HEAD_DIM, LANES)
+                ref[place, pl.ds(to, LANES)] = pair.astype(bf16)
 
     def backward_chunk(g, chunks):
         starts = [pl.multiple_of(i * LANES, LANES) for i in chunks]
@@ -381,7 +390,7 @@
             acc[g, part, :] += mul(cat[part, :], everything)
         for u, i in enumerate(chunks):
             at = u * 2 * LANES
-            turned = mul(kvt[:HEAD_DIM, :], cat[:, at : at + LANES])
+            turned = mul(kvt[g], cat[:, at : at + LANES])
             put_heads(g, i, turned.T * scale_by, gq_my, gq_send)
 
     def forward_chunk(g, chunks):
@@ -404,7 +413,7 @@
             inverse = 1.0 / norm_sum
             for part in parts:
                 cat[part, u * LANES : (u + 1) * LANES] = (ex[u, part, :] * inverse).astype(bf16)
-        turned = mul(kvt[HEAD_DIM:, :], cat[:, : len(chunks) * LANES])
+        turned = mul(kvt[g], cat[:, : len(chunks) * LANES])
         for u, i in enumerate(chunks):
             put_heads(g, i, turned[:, u * LANES : (u + 1) * LANES].T, mix_my, mix_send)
 
@@ -417,28 +426,27 @@
 
         lax.fori_loop(begin, end, body, 0)
 
-    def turn(kv_ref, g):
-        kvt[...] = kv_ref[g].astype(f32).T.astype(bf16)
+    def turn(kv_ref, g, first):
+        whole = kv_ref[g].astype(f32).T
+        kvt[g] = whole[first : first + HEAD_DIM, :].astype(bf16)
 
     def after_first():
-        hop_kv(kvb, 0, 1)
-        send_kv(kvf, 1, 0)
-
-    def after_sums():
         hop_kv(kvf, 1, 0)
         send_kv(kvf, 1, 1)
 
     backward_actions = [
-        {1: after_first},
-        {0: after_sums, 1: lambda: hop_sums(0), 2: lambda: hop_kv(kvf, 1, 1)},
+        {0: lambda: send_kv(kvf, 1, 0), 1: lambda: hop_kv(kvb, 0, 1), 2: after_first},
+        {1: lambda: hop_kv(kvf, 1, 1), 2: lambda: hop_sums(0)},
     ]
     for g in range(LOCAL):
         kv_arrived(kvb, 0, g, g == 0)
-        turn(kvb, g)
+        turn(kvb, g, 0)
         acc[g] = jnp.zeros((total, LANES), f32)
         run(backward_chunk, g, 0, rounds, backward_actions[g])
         send_sums(g)
     pair_copy(3, gq_send, gq_recv)
+    pair_arrived(1, qx_recv.at[1])
+    spread(qx_recv[1], qf, 1, False, scale_by)
 
     def shift(at, src, dst, where, begin, end, edge, arrive_edge):
         def copy(index, first, stop):
@@ -471,7 +479,14 @@
 
         return finish
 
-    def project_out(at, begin, end):
+    def forward_part(at):
+        begin, end = at * UNROLL * slab, (at + 1) * UNROLL * slab
+
+        def body(g, carry):
+            forward_chunk(g, [at * UNROLL + u for u in range(UNROLL)])
+            return carry
+
+        lax.fori_loop(0, LOCAL, body, 0)
         place = slice(begin, end)
         pair_copy(4 + at, mix_send.at[place], mix_recv.at[place])
         made = xf[place, :].astype(f32) + mul(mix_my[place, :], wo[my_cols, :])
@@ -481,12 +496,11 @@
         return shift(at, of, outf_h, after, begin, end, sections - 1, 0)
 
     for g in range(LOCAL):
-        if g == 1:
-            hop_sums(1)
         kv_arrived(kvf, 1, g)
-        turn(kvf, g)
-        run(forward_chunk, g, 0, early, {})
-    finish_early = project_out(0, 0, cut)
+        turn(kvf, g, HEAD_DIM)
+    finishes = [forward_part(0)]
+    hop_sums(1)
+    finishes.append(forward_part(1))
 
     for g in range(LOCAL):
         own = acc[g, pl.ds(member * rows, rows), :]
@@ -526,12 +540,10 @@
         pushed - plain * jnp.mean(pushed * plain, axis=-1, keepdims=True)
     )
     ob[...] = grad_in.astype(bf16)
-    finish_b = shift(2, ob, outb_h, before, 0, rows, 0, sections - 1)
-
-    for g in range(LOCAL):
-        turn(kvf, g)
-        run(forward_chunk, g, early, rounds, {})
-    finish_late = project_out(1, cut, rows)
+    finish_b = shift(rounds, ob, outb_h, before, 0, rows, 0, sections - 1)
+
+    for part in range(2, rounds):
+        finishes.append(forward_part(part))
 
     for copy in pair_copies:
         copy.wait_send()
@@ -539,8 +551,8 @@
     finish_kv(kvf, 1)
     for g in range(LOCAL):
         finish_sums(g)
-    finish_early()
-    finish_late()
+    for finish in finishes:
+        finish()
     finish_b()
 
 
@@ -553,6 +565,7 @@
     total = GROUP * rows
     stack = SHARED * both
     half = width // PAIR
+    rounds = stack // LANES // UNROLL
     anywhere = pl.BlockSpec(memory_space=pl.ANY)
     far_memory = pl.BlockSpec(memory_space=pltpu.HBM)
     block = jax.ShapeDtypeStruct((rows, width), bf16)
@@ -569,7 +582,7 @@
             vmem(w_query.shape[1:], bf16), vmem(w_keyval.shape[1:], bf16), vmem(w_out.shape[1:], bf16),
             vmem((rows, width), bf16),
             vmem((LOCAL, total, LANES), bf16), vmem((LOCAL, total, LANES), bf16),
-            vmem((LANES, total), bf16),
+            vmem((LOCAL, HEAD_DIM, total), bf16),
             vmem((LOCAL, stack, LANES), bf16), vmem((LOCAL, stack, LANES), bf16),
             vmem((LOCAL, stack, LANES), bf16),
             vmem((total, LANES), jnp.int32),
@@ -582,10 +595,10 @@
             vmem((rows, half), bf16), vmem((rows, half), bf16), vmem((rows, half), bf16),
             vmem((rows, half), bf16), vmem((rows, half), bf16), vmem((rows, half), bf16),
             vmem((rows, width), bf16), vmem((rows, width), bf16),
-            dma((7,)), dma((6,)), dma((6,)),
+            dma((7,)), dma((4 + rounds,)), dma((4 + rounds,)),
             dma((2, LOCAL, GROUP)), dma((2, LOCAL, GROUP)),
             dma((LOCAL, GROUP)), dma((LOCAL, GROUP)),
-            dma((3, 2)), dma((3, 2)),
+            dma((rounds + 1, 2)), dma((rounds + 1, 2)),
             dma((3, LOCAL)), dma((3, LOCAL)),
         ],
         compiler_params=pltpu.CompilerParams(

time: 56.2 us -> 52.6 us (0.936)
  Pallas kernels: 52.9 us -> 49.5 us
    pallas_call x1, Pallas kernels: 52.9 us -> 49.5 us  [shards(): pl.pallas_call(functools.partial(kernel, sections, mem), out_shape=(block...]
where the time goes in v2:
time: 52.6 us; the launch traced here: 52.3 us
  Pallas kernels  49.5 us (94%)
  other arithmetic  2.09 us (4%)
  between operations  0.69 us (1%)
    pallas_call x1, Pallas kernels, shards(): pl.pallas_call(functools.partial(kernel, sections, mem), out_shape=(block...  49.5 us
    broadcast_in_dim x1, other arithmetic, shards(): jnp.where(token_row & (section_now == sections - 1), edge, returned)[None]  2.07 us

profile of v2, /device:TPU:5, one launch (start us, length us, event | category | flops | bytes accessed | tf_op | source)
XLA Modules:
  0.0 52.3 jit_solution(9423435242392974225)
XLA Ops:
  0.7 0.0 copy-start
  0.7 0.0 copy-start.1
  0.7 49.5 %shard_map.104 = (bf16[144,1024]{1,0:T(8,128)(2,1)}, bf16[144,1024]{1,0:T(8,128)(2,1)}) custom-call(bf16[144,1024]{1,0:T(8,128)(2,1)} %bitcast.13, bf16[144,1024]{1,0:T(8,128)(2,1)} %bitcast.14, bf16[144,1024]{1,0:T(8,128)(2,1)} %bitcast.15, bf16[1,1024]{1,0:T(2,128)(2,1)} %gain_h.1, bf16[1024,1024]{1,0:T(8,128)(2,1)} %bitcast.10, ...), custom_call_target="tpu_custom_call" | custom-call | tf_op jit(solution)/shard_map/pallas_call | solution.py:574
  50.2 0.0 copy-done
  50.2 0.0 copy-done.1
  50.3 2.1 %select_bitcast_fusion = (bf16[1,144,1024]{2,1,0:T(8,128)(2,1)}, bf16[1,144,1024]{2,1,0:T(8,128)(2,1)}) fusion(bf16[144,1024]{1,0:T(8,128)(2,1)} %get-tuple-element.5, bf16[128,1024]{1,0:T(8,128)(2,1)S(1)} %copy-done, pred[144]{0:T(512)(128)(4,1)S(1)} %fusion, bf16[144,1024]{1,0:T(8,128)(2,1)} %get-tuple-element.4, bf16[128,1024]{1,0:T(8,128)(2,1)S(1)} %copy-done.1, ...), kind=kLoop, calls=%fused_computation | loop fusion | flops 294912 | bytes 1704224 | tf_op jit(solution)/shard_map/broadcast_in_dim | solution.py:612
  (2 shorter events, 0.0 us)
Async XLA Ops:
  0.7 49.6 %copy-start = (bf16[128,1024]{1,0:T(8,128)(2,1)S(1)}, bf16[128,1024]{1,0:T(8,128)(2,1)}, u32[]{:S(2)}) copy-start(bf16[128,1024]{1,0:T(8,128)(2,1)} %param.13) | copy-start | bytes 786436
  0.7 49.6 %copy-start.1 = (bf16[128,1024]{1,0:T(8,128)(2,1)S(1)}, bf16[128,1024]{1,0:T(8,128)(2,1)}, u32[]{:S(2)}) copy-start(bf16[128,1024]{1,0:T(8,128)(2,1)} %param.12) | copy-start | bytes 786436

commit v3 on v2

--- a/solution.py
+++ b/solution.py
@@ -17,10 +17,13 @@
 SHARED = HEADS // KV_HEADS
 LANES = 128
 PIECES = 4
+SPLIT = 2
+FOLD = 8
 UNROLL = 3
 
 epsilon = 1e-05
 far = 1 << 30
+wide = 3e38
 
 bf16 = jnp.bfloat16
 f32 = jnp.float32
@@ -36,11 +39,11 @@
     sections, mem,
     xf_h, xb_h, cot_h, gain_h, wq_h, wkv_h, wo_h,
     outf_h, outb_h,
-    xf, xb, cot, gain_v, wq, wkv, wo, normed, kvf, kvb, kvt, qf, qb, gb, kpos,
+    xf, xb, cot, gain_v, wq, wkv, wo, normed, kvf, kvb, kvt, qf, qb, gb, bias,
     sd, ex, cat, acc, gsend, grecv, gpass, gsum, kvown, qx_send, qx_recv,
-    gq_my, gq_send, gq_recv, mix_my, mix_send, mix_recv, of, ob,
+    gq_my, gq_send, gq_recv, mix_my, mix_send, mix_recv, of, ob, via_f, via_b, early,
     local_sem, pair_send, pair_recv, kv_send, kv_recv, gr_send, gr_recv, sec_send, sec_recv,
-    hop_send, hop_recv,
+    hop_send, hop_recv, via_send, via_recv,
 ):
     rows = xf_h.shape[0]
     width = xf_h.shape[1]
@@ -68,7 +71,11 @@
             barrier, inc=1, device_id={"ctx": base + lax.rem(member + k, GROUP)},
             device_id_type=pl.DeviceIdType.MESH,
         )
-    for neighbour in (after, before):
+    detour = sections == PAIR * PAIR
+    greeted = [after, before]
+    if detour:
+        greeted.append(lax.rem(section + PAIR, sections))
+    for neighbour in greeted:
         pl.semaphore_signal(
             barrier, inc=1, device_id={"section": neighbour},
             device_id_type=pl.DeviceIdType.MESH,
@@ -101,12 +108,6 @@
 
     def pair_arrived(at, dst):
         remote(dst, dst, pair_send.at[at], pair_recv.at[at], {"ctx": partner}).wait_recv()
-
-    for b in range(GROUP):
-        inner = lax.broadcasted_iota(jnp.int32, (rows, LANES), 0)
-        kpos[b * rows : (b + 1) * rows, :] = jnp.where(
-            inner < mem, -1, b * tokens + inner - mem
-        )
 
     def norm(x):
         values = x.astype(f32)
@@ -305,12 +306,28 @@
         qx_send[at] = mul(normed[...], wq[:, their_cols]).astype(bf16)
         spread(mul(normed[...], wq[:, my_cols]).astype(bf16), q_ref, 0, False, scale_by)
 
+    big = total // PIECES
+    step = big // SPLIT
+
+    def make_bias():
+        lane = lax.broadcasted_iota(jnp.int32, (1, LANES), 1)
+        block = jnp.where(lane < LANES // PAIR, member, chip * PAIR + other)
+        key = lax.broadcasted_iota(jnp.int32, (rows, LANES), 0)
+        for i in range(rows // slab):
+            inner = i * slab + lax.rem(lane, slab)
+            position = jnp.where(inner < mem, far, block * tokens + inner - mem)
+            for b in range(GROUP):
+                place = jnp.where(key < mem, -1, b * tokens + key - mem)
+                bias[i, b * rows : (b + 1) * rows, :] = jnp.where(place <= position, wide, -1e30)
+
+    parts = [slice(p * step, (p + 1) * step) for p in range(PIECES * SPLIT)]
+
     load_xb.wait()
     load_gain.wait()
     make_normed(xb)
     load_wkv.wait()
     project_kv(kvb, 0)
-    pl.semaphore_wait(barrier, GROUP + 1)
+    pl.semaphore_wait(barrier, GROUP - 1 + len(greeted))
     send_kv(kvb, 0, 0, 0)
     load_wq.wait()
     make_query(0, qb)
@@ -333,16 +350,7 @@
     send_kv(kvb, 0, 1)
     make_query(1, qf)
     pair_copy(1, qx_send.at[1], qx_recv.at[1])
-
-    step = total // PIECES
-
-    def query_positions(i):
-        lane = lax.broadcasted_iota(jnp.int32, (1, LANES), 1)
-        block = jnp.where(lane < LANES // PAIR, member, chip * PAIR + other)
-        inner = i * slab + lax.rem(lane, slab)
-        return jnp.where(inner < mem, far, block * tokens + inner - mem)
-
-    parts = [slice(p * step, (p + 1) * step) for p in range(PIECES)]
+    make_bias()
 
     def put_heads(g, i, turned, mine_ref, theirs_ref):
         place = pl.ds(pl.multiple_of(i * slab, slab), slab)
@@ -355,6 +363,16 @@
                 to = pl.multiple_of((g * SHARED + h) * HEAD_DIM, LANES)
                 ref[place, pl.ds(to, LANES)] = pair.astype(bf16)
 
+    def folded(x):
+        return x.reshape(step // FOLD, FOLD, LANES)
+
+    def combine(tops, sums):
+        top = functools.reduce(jnp.maximum, tops)
+        top = jnp.max(top, axis=0, keepdims=True)
+        weights = [jnp.exp(t - top) for t in tops]
+        norm_sum = sum(w * s for w, s in zip(weights, sums))
+        return weights, 1.0 / jnp.sum(norm_sum, axis=0, keepdims=True)
+
     def backward_chunk(g, chunks):
         starts = [pl.multiple_of(i * LANES, LANES) for i in chunks]
         pairs = [
@@ -362,29 +380,31 @@
             for at in starts
         ]
         for u, i in enumerate(chunks):
-            position = query_positions(i)
-            top = None
-            for part in parts:
-                product = mul(kvb[g, part, :], pairs[u], NT)
-                scores = jnp.where(kpos[part, :] <= position, product[:, :LANES], -1e30)
-                sd[u, part, :LANES] = scores
-                sd[u, part, LANES:] = product[:, LANES:]
-                peak = jnp.max(scores, axis=0, keepdims=True)
-                top = peak if top is None else jnp.maximum(top, peak)
-            norm_sum = jnp.zeros((1, LANES), f32)
-            delta = jnp.zeros((1, LANES), f32)
-            for part in parts:
-                expd = jnp.exp(sd[u, part, :LANES] - top)
-                ex[u, part, :] = expd
-                norm_sum += jnp.sum(expd, axis=0, keepdims=True)
-                delta += jnp.sum(expd * sd[u, part, LANES:], axis=0, keepdims=True)
-            inverse = 1.0 / norm_sum
-            delta = delta * inverse
+            tops, sums, dots = [], [], []
+            products = [
+                mul(kvb[g, p * big : (p + 1) * big, :], pairs[u], NT) for p in range(PIECES)
+            ]
+            for at, part in enumerate(parts):
+                within = at % SPLIT * step
+                product = products[at // SPLIT][within : within + step, :]
+                scores = folded(jnp.minimum(product[:, :LANES], bias[i, part, :]))
+                top = jnp.max(scores, axis=0)
+                expd = jnp.exp(scores - top)
+                rates = folded(product[:, LANES:])
+                ex[u, part, :] = expd.reshape(step, LANES)
+                sd[u, part, :] = rates.reshape(step, LANES)
+                tops.append(top)
+                sums.append(jnp.sum(expd, axis=0))
+                dots.append(jnp.sum(expd * rates, axis=0))
+            weights, inverse = combine(tops, sums)
+            delta = sum(w * d for w, d in zip(weights, dots))
+            delta = jnp.sum(delta, axis=0, keepdims=True) * inverse
             at = u * 2 * LANES
-            for part in parts:
-                probs = ex[u, part, :] * inverse
-                cat[part, at + LANES : at + 2 * LANES] = probs.astype(bf16)
-                cat[part, at : at + LANES] = (probs * (sd[u, part, LANES:] - delta)).astype(bf16)
+            for part, weight in zip(parts, weights):
+                probs = folded(ex[u, part, :]) * (weight * inverse)
+                dscores = probs * (folded(sd[u, part, :]) - delta)
+                cat[part, at + LANES : at + 2 * LANES] = probs.reshape(step, LANES).astype(bf16)
+                cat[part, at : at + LANES] = dscores.reshape(step, LANES).astype(bf16)
         everything = jnp.concatenate(pairs, axis=0)
         for part in parts:
             acc[g, part, :] += mul(cat[part, :], everything)
@@ -397,22 +417,23 @@
         for u, i in enumerate(chunks):
             start = pl.multiple_of(i * LANES, LANES)
             queries = qf[g, pl.ds(start, LANES), :]
-            position = query_positions(i)
-            top = None
-            for part in parts:
-                product = mul(kvf[g, part, :], queries, NT)
-                scores = jnp.where(kpos[part, :] <= position, product, -1e30)
-                sd[u, part, :LANES] = scores
-                peak = jnp.max(scores, axis=0, keepdims=True)
-                top = peak if top is None else jnp.maximum(top, peak)
-            norm_sum = jnp.zeros((1, LANES), f32)
-            for part in parts:
-                expd = jnp.exp(sd[u, part, :LANES] - top)
-                ex[u, part, :] = expd
-                norm_sum += jnp.sum(expd, axis=0, keepdims=True)
-            inverse = 1.0 / norm_sum
-            for part in parts:
-                cat[part, u * LANES : (u + 1) * LANES] = (ex[u, part, :] * inverse).astype(bf16)
+            tops, sums = [], []
+            products = [
+                mul(kvf[g, p * big : (p + 1) * big, :], queries, NT) for p in range(PIECES)
+            ]
+            for at, part in enumerate(parts):
+                within = at % SPLIT * step
+                product = products[at // SPLIT][within : within + step, :]
+                scores = folded(jnp.minimum(product, bias[i, part, :]))
+                top = jnp.max(scores, axis=0)
+                expd = jnp.exp(scores - top)
+                ex[u, part, :] = expd.reshape(step, LANES)
+                tops.append(top)
+                sums.append(jnp.sum(expd, axis=0))
+            weights, inverse = combine(tops, sums)
+            for part, weight in zip(parts, weights):
+                probs = folded(ex[u, part, :]) * (weight * inverse)
+                cat[part, u * LANES : (u + 1) * LANES] = probs.reshape(step, LANES).astype(bf16)
         turned = mul(kvt[g], cat[:, : len(chunks) * LANES])
         for u, i in enumerate(chunks):
             put_heads(g, i, turned[:, u * LANES : (u + 1) * LANES].T, mix_my, mix_send)
@@ -434,8 +455,12 @@
         hop_kv(kvf, 1, 0)
         send_kv(kvf, 1, 1)
 
+    def at_start():
+        hop_kv(kvb, 0, 1)
+        send_kv(kvf, 1, 0)
+
     backward_actions = [
-        {0: lambda: send_kv(kvf, 1, 0), 1: lambda: hop_kv(kvb, 0, 1), 2: after_first},
+        {0: at_start, 2: after_first},
         {1: lambda: hop_kv(kvf, 1, 1), 2: lambda: hop_sums(0)},
     ]
     for g in range(LOCAL):
@@ -448,28 +473,62 @@
     pair_arrived(1, qx_recv.at[1])
     spread(qx_recv[1], qf, 1, False, scale_by)
 
-    def shift(at, src, dst, where, begin, end, edge, arrive_edge):
-        def copy(index, first, stop):
-            place = pl.ds(first, stop - first)
+    def shift(at, src, dst, via, where, begin, end, edge, arrive_edge, turning, target):
+        place = pl.ds(max(begin, mem), end - max(begin, mem))
+
+        def copy(index, one):
             return remote(
-                src.at[place], dst.at[place],
+                src.at[one], dst.at[one],
                 sec_send.at[at, index], sec_recv.at[at, index], {"section": where},
             )
 
-        small = copy(0, begin, mem) if begin < mem else None
-        large = copy(1, max(begin, mem), end)
+        small = copy(0, pl.ds(begin, mem - begin)) if begin < mem else None
+        large = copy(1, place)
+        around = remote(
+            src.at[place], via.at[place], via_send.at[at], via_recv.at[at], {"section": edge}
+        )
+        onward = remote(
+            via.at[place], dst.at[place],
+            sec_send.at[at, 1], sec_recv.at[at, 1], {"section": target},
+        )
+        if detour:
+            turns = jnp.logical_and(section == turning, core == 1)
+            passes = jnp.logical_and(section == edge, core == 1)
         if small is not None:
             small.start()
-
-        @pl.when(section != edge)
+        straight = section != edge
+        if detour:
+            straight = jnp.logical_and(straight, jnp.logical_not(turns))
+
+            @pl.when(turns)
+            def _():
+                around.start()
+
+        @pl.when(straight)
         def _():
             large.start()
+
+        def pass_on():
+            if detour:
+                @pl.when(passes)
+                def _():
+                    around.wait_recv()
+                    onward.start()
 
         def finish():
             if small is not None:
                 small.wait()
 
-            @pl.when(section != edge)
+            if detour:
+                @pl.when(turns)
+                def _():
+                    around.wait_send()
+
+                @pl.when(passes)
+                def _():
+                    onward.wait_send()
+
+            @pl.when(straight)
             def _():
                 large.wait_send()
 
@@ -477,30 +536,41 @@
             def _():
                 large.wait_recv()
 
-        return finish
-
-    def forward_part(at):
+        return pass_on, finish
+
+    def attend(g, at):
+        forward_chunk(g, [at * UNROLL + u for u in range(UNROLL)])
+        if g == LOCAL - 1:
+            place = slice(at * UNROLL * slab, (at + 1) * UNROLL * slab)
+            pair_copy(4 + at, mix_send.at[place], mix_recv.at[place])
+
+    def project_out(at):
         begin, end = at * UNROLL * slab, (at + 1) * UNROLL * slab
-
-        def body(g, carry):
-            forward_chunk(g, [at * UNROLL + u for u in range(UNROLL)])
-            return carry
-
-        lax.fori_loop(0, LOCAL, body, 0)
         place = slice(begin, end)
-        pair_copy(4 + at, mix_send.at[place], mix_recv.at[place])
         made = xf[place, :].astype(f32) + mul(mix_my[place, :], wo[my_cols, :])
         pair_arrived(4 + at, mix_recv.at[place])
         made += mul(mix_recv[place, :], wo[their_cols, :])
         of[place, :] = made.astype(bf16)
-        return shift(at, of, outf_h, after, begin, end, sections - 1, 0)
-
-    for g in range(LOCAL):
-        kv_arrived(kvf, 1, g)
-        turn(kvf, g, HEAD_DIM)
-    finishes = [forward_part(0)]
+        return shift(
+            at, of, outf_h, via_f, after, begin, end, sections - 1, 0,
+            sections // PAIR - 1, sections // PAIR,
+        )
+
+    kv_arrived(kvf, 1, 0)
+    turn(kvf, 0, HEAD_DIM)
+    attend(0, 0)
+    attend(0, 1)
+    kv_arrived(kvf, 1, 1)
+    turn(kvf, 1, HEAD_DIM)
+    attend(1, 0)
     hop_sums(1)
-    finishes.append(forward_part(1))
+    pair_arrived(3, gq_recv)
+    early[...] = mul(gq_my[...], wq[:, my_cols], NT) + mul(gq_recv[...], wq[:, their_cols], NT)
+    moves = [project_out(0)]
+    attend(1, 1)
+    attend(0, 2)
+    moves[0][0]()
+    moves.append(project_out(1))
 
     for g in range(LOCAL):
         own = acc[g, pl.ds(member * rows, rows), :]
@@ -526,13 +596,10 @@
                 cross = value if cross is None else cross + value
         gsum[core * LOCAL + g] = own
         gsum[other * LOCAL + g] = cross
-    pair_arrived(3, gq_recv)
     columns = [gsum[h, :, :HEAD_DIM] for h in range(KV_HEADS)]
     columns += [gsum[h, :, HEAD_DIM:] for h in range(KV_HEADS)]
     grad_kv = jnp.concatenate(columns, axis=1).astype(bf16)
-    grad_normed = mul(grad_kv, wkv[...], NT)
-    grad_normed += mul(gq_my[...], wq[:, my_cols], NT)
-    grad_normed += mul(gq_recv[...], wq[:, their_cols], NT)
+    grad_normed = early[...] + mul(grad_kv, wkv[...], NT)
     values, scale = norm(xb[...])
     plain = values * scale
     pushed = gain_v[...].astype(f32) * grad_normed
@@ -540,10 +607,20 @@
         pushed - plain * jnp.mean(pushed * plain, axis=-1, keepdims=True)
     )
     ob[...] = grad_in.astype(bf16)
-    finish_b = shift(rounds, ob, outb_h, before, 0, rows, 0, sections - 1)
-
-    for part in range(2, rounds):
-        finishes.append(forward_part(part))
+    backs = [
+        shift(
+            rounds + p, ob, outb_h, via_b, before, p * UNROLL * slab, (p + 1) * UNROLL * slab,
+            0, sections - 1, sections // PAIR, sections // PAIR - 1,
+        )
+        for p in range(rounds)
+    ]
+    attend(1, 2)
+    moves[1][0]()
+    moves.append(project_out(2))
+    for pass_on, _ in backs:
+        pass_on()
+    moves[2][0]()
+    moves += backs
 
     for copy in pair_copies:
         copy.wait_send()
@@ -551,9 +628,8 @@
     finish_kv(kvf, 1)
     for g in range(LOCAL):
         finish_sums(g)
-    for finish in finishes:
+    for _, finish in moves:
         finish()
-    finish_b()
 
 
 def shards(fwd_in, bwd_saved, bwd_cot, new_tokens, loss_cot, gain, w_query, w_keyval, w_out):
@@ -585,8 +661,8 @@
             vmem((LOCAL, HEAD_DIM, total), bf16),
             vmem((LOCAL, stack, LANES), bf16), vmem((LOCAL, stack, LANES), bf16),
             vmem((LOCAL, stack, LANES), bf16),
-            vmem((total, LANES), jnp.int32),
-            vmem((UNROLL, total, 2 * LANES), f32), vmem((UNROLL, total, LANES), f32),
+            vmem((rows * PAIR * SHARED // LANES, total, LANES), f32),
+            vmem((UNROLL, total, LANES), f32), vmem((UNROLL, total, LANES), f32),
             vmem((total, UNROLL * 2 * LANES), bf16),
             vmem((LOCAL, total, LANES), f32), vmem((LOCAL, total, LANES), bf16),
             vmem((GROUP, LOCAL, rows, LANES), bf16), vmem((LOCAL, both, LANES), bf16),
@@ -595,14 +671,16 @@
             vmem((rows, half), bf16), vmem((rows, half), bf16), vmem((rows, half), bf16),
             vmem((rows, half), bf16), vmem((rows, half), bf16), vmem((rows, half), bf16),
             vmem((rows, width), bf16), vmem((rows, width), bf16),
+            vmem((rows, width), bf16), vmem((rows, width), bf16), vmem((rows, width), f32),
             dma((7,)), dma((4 + rounds,)), dma((4 + rounds,)),
             dma((2, LOCAL, GROUP)), dma((2, LOCAL, GROUP)),
             dma((LOCAL, GROUP)), dma((LOCAL, GROUP)),
-            dma((rounds + 1, 2)), dma((rounds + 1, 2)),
+            dma((2 * rounds, 2)), dma((2 * rounds, 2)),
             dma((3, LOCAL)), dma((3, LOCAL)),
+            dma((2 * rounds,)), dma((2 * rounds,)),
         ],
         compiler_params=pltpu.CompilerParams(
-            collective_id=0, has_side_effects=True, vmem_limit_bytes=60500 * 1024
+            collective_id=0, has_side_effects=True, vmem_limit_bytes=54500 * 1024
         ),
     )(fwd_in[0], bwd_saved[0], bwd_cot[0], gain, w_query[0], w_keyval[0], w_out[0])
     token_row = lax.broadcasted_iota(jnp.int32, (rows, 1), 0) >= mem

time: 52.6 us -> 49.8 us (0.947)
  Pallas kernels: 49.5 us -> 47.2 us
  other arithmetic: 2.09 us -> 1.03 us
  local copies, waits for them, and re-layouts: 0.01 us -> 0.69 us
    pallas_call x1, Pallas kernels: 49.5 us -> 47.2 us  [shards(): pl.pallas_call(functools.partial(kernel, sections, mem), out_shape=(block...]
    broadcast_in_dim x1, other arithmetic: 2.07 us -> 1.02 us  [shards(): jnp.where(token_row & (section_now == sections - 1), edge, returned)[None]]
    unnamed x4 -> x6, local copies, waits for them, and re-layouts: 0.01 us -> 0.69 us
where the time goes in v3:
time: 49.8 us; the launch traced here: 49.6 us
  Pallas kernels  47.2 us (95%)
  other arithmetic  1.03 us (2%)
  local copies, waits for them, and re-layouts  0.69 us (1%)
  between operations  0.68 us (1%)
    pallas_call x1, Pallas kernels, shards(): pl.pallas_call(functools.partial(kernel, sections, mem), out_shape=(block...  47.2 us
    broadcast_in_dim x1, other arithmetic, shards(): jnp.where(token_row & (section_now == sections - 1), edge, returned)[None]  1.02 us

profile of v3, /device:TPU:5, one launch (start us, length us, event | category | flops | bytes accessed | tf_op | source)
XLA Modules:
  0.0 49.6 jit_solution(12982317488273449915)
XLA Ops:
  0.7 0.0 copy-start
  0.7 0.7 %copy-done = bf16[1,1024]{1,0:T(2,128)(2,1)S(1)} copy-done((bf16[1,1024]{1,0:T(2,128)(2,1)S(1)}, bf16[1,1024]{1,0:T(2,128)(2,1)}, u32[]{:S(2)}) %copy-start) | copy-done | bytes 2072
  1.4 0.0 copy-start.1
  1.4 0.0 copy-start.2
  1.4 47.2 %shard_map.104 = (bf16[144,1024]{1,0:T(8,128)(2,1)S(1)}, bf16[144,1024]{1,0:T(8,128)(2,1)S(1)}) custom-call(bf16[144,1024]{1,0:T(8,128)(2,1)} %bitcast.13, bf16[144,1024]{1,0:T(8,128)(2,1)} %bitcast.14, bf16[144,1024]{1,0:T(8,128)(2,1)} %bitcast.15, bf16[1,1024]{1,0:T(2,128)(2,1)S(1)} %copy-done, bf16[1024,1024]{1,0:T(8,128)(2,1)} %bitcast.10, ...), custom_call_target="tpu_custom_call" | custom-call | tf_op jit(solution)/shard_map/pallas_call | solution.py:650
  48.6 0.0 copy-done.1
  48.6 0.0 copy-done.2
  48.6 1.0 %select_bitcast_fusion = (bf16[1,144,1024]{2,1,0:T(8,128)(2,1)}, bf16[1,144,1024]{2,1,0:T(8,128)(2,1)}) fusion(bf16[144,1024]{1,0:T(8,128)(2,1)S(1)} %get-tuple-element.5, bf16[128,1024]{1,0:T(8,128)(2,1)S(1)} %copy-done.1, pred[144]{0:T(512)(128)(4,1)S(1)} %fusion, bf16[144,1024]{1,0:T(8,128)(2,1)S(1)} %get-tuple-element.4, ...), kind=kLoop, calls=%fused_computation | loop fusion | flops 294912 | bytes 1704224 | tf_op jit(solution)/shard_map/broadcast_in_dim | solution.py:690
  (2 shorter events, 0.0 us)
Async XLA Ops:
  0.7 0.7 %copy-start = (bf16[1,1024]{1,0:T(2,128)(2,1)S(1)}, bf16[1,1024]{1,0:T(2,128)(2,1)}, u32[]{:S(2)}) copy-start(bf16[1,1024]{1,0:T(2,128)(2,1)} %gain_h.1) | copy-start | bytes 6148
  1.4 47.2 %copy-start.1 = (bf16[128,1024]{1,0:T(8,128)(2,1)S(1)}, bf16[128,1024]{1,0:T(8,128)(2,1)}, u32[]{:S(2)}) copy-start(bf16[128,1024]{1,0:T(8,128)(2,1)} %param.13) | copy-start | bytes 786436
  1.4 47.2 %copy-start.2 = (bf16[128,1024]{1,0:T(8,128)(2,1)S(1)}, bf16[128,1024]{1,0:T(8,128)(2,1)}, u32[]{:S(2)}) copy-start(bf16[128,1024]{1,0:T(8,128)(2,1)} %param.12) | copy-start | bytes 786436

commit v4 on v3

--- a/solution.py
+++ b/solution.py
@@ -153,12 +153,19 @@
         for g in range(LOCAL):
             kv_ref[g, pl.ds(member * rows, rows), :] = kvown[kind, core * LOCAL + g]
 
+    def early_class(src, dst):
+        ends = jnp.logical_or(dst == 0, dst == last)
+        near = jnp.where(dst == 0, 1, last - 1)
+        across = jnp.where(dst == 1, last, 0)
+        return jnp.where(src == jnp.where(ends, near, across), 1, 0)
+
     def kv_copy(kv_ref, kind, g, k):
         to = peer(k)
         return remote(
             kvown.at[kind, lax.rem(to, PAIR) * LOCAL + g],
             kv_ref.at[g, pl.ds(member * rows, rows)],
-            kv_send.at[kind, g, k], kv_recv.at[kind, g, k], {"ctx": base + to},
+            kv_send.at[kind, g], kv_recv.at[kind, g, early_class(chip, to // PAIR)],
+            {"ctx": base + to},
         )
 
     def is_first(one):
@@ -177,12 +184,19 @@
             def _():
                 kv_copy(kv_ref, kind, g, k).start()
 
+    def by_place(at_end, at_middle, action):
+        pl.when(is_end)(lambda: action(at_end))
+        pl.when(is_middle)(lambda: action(at_middle))
+
     def finish_kv(kv_ref, kind):
         for g in range(LOCAL):
-            for k in order:
-                @pl.when(jnp.logical_not(is_far(peer(k))))
-                def _():
-                    kv_copy(kv_ref, kind, g, k).wait_send()
+            def wait(count):
+                place = kv_ref.at[g, pl.ds(0, count * rows)]
+                remote(
+                    place, place, kv_send.at[kind, g], kv_recv.at[kind, g, 0], {"ctx": partner}
+                ).wait_send()
+
+            by_place(GROUP - 1 - PAIR, GROUP - 1, wait)
 
             @pl.when(is_middle)
             def _():
@@ -195,36 +209,30 @@
             {"ctx": base + hop_to * PAIR + core},
         )
 
-    def kv_wait(kv_ref, kind, g, one):
-        k = lax.rem(member + GROUP - one, GROUP)
-        place = kv_ref.at[g, pl.ds(one * rows, rows)]
+    def kv_wait(kv_ref, kind, g, which, count):
+        place = kv_ref.at[g, pl.ds(0, count * rows)]
         remote(
-            place, place, kv_send.at[kind, g, k], kv_recv.at[kind, g, k], {"ctx": base + one}
+            place, place, kv_send.at[kind, g], kv_recv.at[kind, g, which], {"ctx": partner}
         ).wait_recv()
 
     def hop_kv(kv_ref, kind, g):
         @pl.when(is_middle)
         def _():
-            for c in range(PAIR):
-                kv_wait(kv_ref, kind, g, hop_from * PAIR + c)
+            kv_wait(kv_ref, kind, g, 1, PAIR)
             hop_copy(kv_ref, kind, g).start()
 
     def near_kv(kv_ref, kind, g):
         @pl.when(is_end)
         def _():
-            for c in range(PAIR):
-                kv_wait(kv_ref, kind, g, adjacent * PAIR + c)
+            kv_wait(kv_ref, kind, g, 1, PAIR)
 
     def kv_arrived(kv_ref, kind, g, near_done=False):
-        for k in range(1, GROUP):
-            one = source(k)
-            done = jnp.logical_and(is_middle, one // PAIR == hop_from)
-            if near_done:
-                done = jnp.logical_or(done, jnp.logical_and(is_end, one // PAIR == adjacent))
-
-            @pl.when(jnp.logical_not(jnp.logical_or(is_far(one), done)))
-            def _():
-                kv_wait(kv_ref, kind, g, one)
+        by_place(
+            GROUP - 1 - 2 * PAIR, GROUP - 1 - PAIR,
+            lambda count: kv_wait(kv_ref, kind, g, 0, count),
+        )
+        if not near_done:
+            near_kv(kv_ref, kind, g)
 
         @pl.when(is_end)
         def _():
@@ -238,7 +246,7 @@
         to = peer(k)
         return remote(
             gsend.at[g, pl.ds(to * rows, rows)], grecv.at[k, g],
-            gr_send.at[g, k], gr_recv.at[g, k], {"ctx": base + to},
+            gr_send.at[g], gr_recv.at[g], {"ctx": base + to},
         )
 
     def is_summed(one):
@@ -280,10 +288,11 @@
         def _():
             sum_copy(g, sum_via).wait_send()
 
-        for k in order:
-            @pl.when(jnp.logical_not(is_far(peer(k))))
-            def _():
-                gr_copy(g, k).wait_send()
+        def wait(count):
+            place = gsend.at[g, pl.ds(0, count * rows)]
+            remote(place, place, gr_send.at[g], gr_recv.at[g], {"ctx": partner}).wait_send()
+
+        by_place(GROUP - 1 - PAIR, GROUP - 1, wait)
 
     def spread(matrix, dst, block, upper, factor):
         rounded = matrix.astype(f32) * factor
@@ -451,23 +460,21 @@
         whole = kv_ref[g].astype(f32).T
         kvt[g] = whole[first : first + HEAD_DIM, :].astype(bf16)
 
-    def after_first():
-        hop_kv(kvf, 1, 0)
-        send_kv(kvf, 1, 1)
-
     def at_start():
         hop_kv(kvb, 0, 1)
         send_kv(kvf, 1, 0)
 
     backward_actions = [
-        {0: at_start, 2: after_first},
-        {1: lambda: hop_kv(kvf, 1, 1), 2: lambda: hop_sums(0)},
+        {0: at_start, 1: lambda: send_kv(kvf, 1, 1), 2: lambda: hop_kv(kvf, 1, 0)},
+        {2: lambda: hop_sums(0)},
     ]
     for g in range(LOCAL):
         kv_arrived(kvb, 0, g, g == 0)
         turn(kvb, g, 0)
         acc[g] = jnp.zeros((total, LANES), f32)
         run(backward_chunk, g, 0, rounds, backward_actions[g])
+        if g == 0:
+            hop_kv(kvf, 1, 1)
         send_sums(g)
     pair_copy(3, gq_send, gq_recv)
     pair_arrived(1, qx_recv.at[1])
@@ -573,6 +580,11 @@
     moves.append(project_out(1))
 
     for g in range(LOCAL):
+        def arrive(count):
+            place = gsend.at[g, pl.ds(0, count * rows)]
+            remote(place, place, gr_send.at[g], gr_recv.at[g], {"ctx": partner}).wait_recv()
+
+        by_place(GROUP - 1 - PAIR, GROUP - 1, arrive)
         own = acc[g, pl.ds(member * rows, rows), :]
         cross = None
         for k in range(1, GROUP):
@@ -581,13 +593,6 @@
             @pl.when(is_far(one))
             def _():
                 grecv[k, g] = jnp.zeros((rows, LANES), bf16)
-
-            @pl.when(jnp.logical_not(is_far(one)))
-            def _():
-                place = grecv.at[k, g]
-                remote(
-                    place, place, gr_send.at[g, k], gr_recv.at[g, k], {"ctx": base + one}
-                ).wait_recv()
 
             value = grecv[k, g].astype(f32)
             if k % PAIR == 0:
@@ -673,8 +678,8 @@
             vmem((rows, width), bf16), vmem((rows, width), bf16),
             vmem((rows, width), bf16), vmem((rows, width), bf16), vmem((rows, width), f32),
             dma((7,)), dma((4 + rounds,)), dma((4 + rounds,)),
-            dma((2, LOCAL, GROUP)), dma((2, LOCAL, GROUP)),
-            dma((LOCAL, GROUP)), dma((LOCAL, GROUP)),
+            dma((2, LOCAL)), dma((2, LOCAL, 2)),
+            dma((LOCAL,)), dma((LOCAL,)),
             dma((2 * rounds, 2)), dma((2 * rounds, 2)),
             dma((3, LOCAL)), dma((3, LOCAL)),
             dma((2 * rounds,)), dma((2 * rounds,)),
@@ -682,7 +687,10 @@
         compiler_params=pltpu.CompilerParams(
             collective_id=0, has_side_effects=True, vmem_limit_bytes=54500 * 1024
         ),
-    )(fwd_in[0], bwd_saved[0], bwd_cot[0], gain, w_query[0], w_keyval[0], w_out[0])
+    )(
+        fwd_in[0], bwd_saved[0], bwd_cot[0], pltpu.with_memory_space_constraint(gain, pltpu.HBM),
+        w_query[0], w_keyval[0], w_out[0],
+    )
     token_row = lax.broadcasted_iota(jnp.int32, (rows, 1), 0) >= mem
     edge = jnp.pad(new_tokens, ((mem, 0), (0, 0)))
     fwd_next = jnp.where(token_row & (section_now == 0), edge, arrived)[None]

time: 49.8 us -> 48.5 us (0.974)
  local copies, waits for them, and re-layouts: 0.69 us -> 0.01 us
  Pallas kernels: 47.2 us -> 46.6 us
    unnamed x6 -> x4, local copies, waits for them, and re-layouts: 0.69 us -> 0.01 us
    pallas_call x1, Pallas kernels: 47.2 us -> 46.6 us  [shards(): pl.pallas_call(functools.partial(kernel, sections, mem), out_shape=(block...]
where the time goes in v4:
time: 48.5 us; the launch traced here: 48.3 us
  Pallas kernels  46.6 us (96%)
  other arithmetic  1.03 us (2%)
  between operations  0.69 us (1%)
    pallas_call x1, Pallas kernels, shards(): pl.pallas_call(functools.partial(kernel, sections, mem), out_shape=(block...  46.6 us
    broadcast_in_dim x1, other arithmetic, shards(): jnp.where(token_row & (section_now == sections - 1), edge, returned)[None]  1.02 us

profile of v4, /device:TPU:5, one launch (start us, length us, event | category | flops | bytes accessed | tf_op | source)
XLA Modules:
  0.0 48.3 jit_solution(4074666126663931048)
XLA Ops:
  0.7 0.0 copy-start
  0.7 0.0 copy-start.1
  0.7 46.6 %shard_map.104 = (bf16[144,1024]{1,0:T(8,128)(2,1)S(1)}, bf16[144,1024]{1,0:T(8,128)(2,1)S(1)}) custom-call(bf16[144,1024]{1,0:T(8,128)(2,1)} %bitcast.13, bf16[144,1024]{1,0:T(8,128)(2,1)} %bitcast.14, bf16[144,1024]{1,0:T(8,128)(2,1)} %bitcast.15, bf16[1,1024]{1,0:T(2,128)(2,1)} %gain_h.1, bf16[1024,1024]{1,0:T(8,128)(2,1)} %bitcast.10, ...), custom_call_target="tpu_custom_call" | custom-call | tf_op jit(solution)/shard_map/pallas_call | solution.py:655
  47.3 0.0 copy-done
  47.3 0.0 copy-done.1
  47.3 1.0 %select_bitcast_fusion = (bf16[1,144,1024]{2,1,0:T(8,128)(2,1)}, bf16[1,144,1024]{2,1,0:T(8,128)(2,1)}) fusion(bf16[144,1024]{1,0:T(8,128)(2,1)S(1)} %get-tuple-element.5, bf16[128,1024]{1,0:T(8,128)(2,1)S(1)} %copy-done, pred[144]{0:T(512)(128)(4,1)S(1)} %fusion, bf16[144,1024]{1,0:T(8,128)(2,1)S(1)} %get-tuple-element.4, bf16[128,1024]{1,0:T(8,128)(2,1)S(1)} %copy-done.1, ...), kind=kLoop, calls=%fused_computation | loop fusion | flops 294912 | bytes 1704224 | tf_op jit(solution)/shard_map/broadcast_in_dim | solution.py:698
  (2 shorter events, 0.0 us)
Async XLA Ops:
  0.7 46.6 %copy-start = (bf16[128,1024]{1,0:T(8,128)(2,1)S(1)}, bf16[128,1024]{1,0:T(8,128)(2,1)}, u32[]{:S(2)}) copy-start(bf16[128,1024]{1,0:T(8,128)(2,1)} %param.13) | copy-start | bytes 786436
  0.7 46.6 %copy-start.1 = (bf16[128,1024]{1,0:T(8,128)(2,1)S(1)}, bf16[128,1024]{1,0:T(8,128)(2,1)}, u32[]{:S(2)}) copy-start(bf16[128,1024]{1,0:T(8,128)(2,1)} %param.12) | copy-start | bytes 786436

commit v5 on v4

--- a/solution.py
+++ b/solution.py
@@ -43,7 +43,7 @@
     sd, ex, cat, acc, gsend, grecv, gpass, gsum, kvown, qx_send, qx_recv,
     gq_my, gq_send, gq_recv, mix_my, mix_send, mix_recv, of, ob, via_f, via_b, early,
     local_sem, pair_send, pair_recv, kv_send, kv_recv, gr_send, gr_recv, sec_send, sec_recv,
-    hop_send, hop_recv, via_send, via_recv,
+    hop_send, hop_recv, via_recv,
 ):
     rows = xf_h.shape[0]
     width = xf_h.shape[1]
@@ -99,15 +99,12 @@
             device_id=where, device_id_type=pl.DeviceIdType.MESH,
         )
 
-    pair_copies = []
-
     def pair_copy(at, src, dst):
-        copy = remote(src, dst, pair_send.at[at], pair_recv.at[at], {"ctx": partner})
-        copy.start()
-        pair_copies.append(copy)
+        group = 0 if at < 3 else min(at - 2, 2)
+        remote(src, dst, pair_send.at[group], pair_recv.at[at], {"ctx": partner}).start()
 
     def pair_arrived(at, dst):
-        remote(dst, dst, pair_send.at[at], pair_recv.at[at], {"ctx": partner}).wait_recv()
+        remote(dst, dst, pair_send.at[0], pair_recv.at[at], {"ctx": partner}).wait_recv()
 
     def norm(x):
         values = x.astype(f32)
@@ -492,7 +489,7 @@
         small = copy(0, pl.ds(begin, mem - begin)) if begin < mem else None
         large = copy(1, place)
         around = remote(
-            src.at[place], via.at[place], via_send.at[at], via_recv.at[at], {"section": edge}
+            src.at[place], via.at[place], sec_send.at[at, 1], via_recv.at[at], {"section": edge}
         )
         onward = remote(
             via.at[place], dst.at[place],
@@ -566,17 +563,17 @@
     kv_arrived(kvf, 1, 0)
     turn(kvf, 0, HEAD_DIM)
     attend(0, 0)
-    attend(0, 1)
     kv_arrived(kvf, 1, 1)
     turn(kvf, 1, HEAD_DIM)
     attend(1, 0)
-    hop_sums(1)
     pair_arrived(3, gq_recv)
     early[...] = mul(gq_my[...], wq[:, my_cols], NT) + mul(gq_recv[...], wq[:, their_cols], NT)
     moves = [project_out(0)]
+    hop_sums(1)
+    attend(0, 1)
     attend(1, 1)
+    moves[0][0]()
     attend(0, 2)
-    moves[0][0]()
     moves.append(project_out(1))
 
     for g in range(LOCAL):
@@ -627,8 +624,10 @@
     moves[2][0]()
     moves += backs
 
-    for copy in pair_copies:
-        copy.wait_send()
+    for group, whole in enumerate((qx_send, gq_send, mix_send)):
+        remote(
+            whole, whole, pair_send.at[group], pair_recv.at[group], {"ctx": partner}
+        ).wait_send()
     finish_kv(kvb, 0)
     finish_kv(kvf, 1)
     for g in range(LOCAL):
@@ -677,12 +676,12 @@
             vmem((rows, half), bf16), vmem((rows, half), bf16), vmem((rows, half), bf16),
             vmem((rows, width), bf16), vmem((rows, width), bf16),
             vmem((rows, width), bf16), vmem((rows, width), bf16), vmem((rows, width), f32),
-            dma((7,)), dma((4 + rounds,)), dma((4 + rounds,)),
+            dma((7,)), dma((3,)), dma((4 + rounds,)),
             dma((2, LOCAL)), dma((2, LOCAL, 2)),
             dma((LOCAL,)), dma((LOCAL,)),
             dma((2 * rounds, 2)), dma((2 * rounds, 2)),
             dma((3, LOCAL)), dma((3, LOCAL)),
-            dma((2 * rounds,)), dma((2 * rounds,)),
+            dma((2 * rounds,)),
         ],
         compiler_params=pltpu.CompilerParams(
             collective_id=0, has_side_effects=True, vmem_limit_bytes=54500 * 1024

time: 48.5 us -> 48.4 us (level)
  no operation moved by 1% of the time
where the time goes in v5:
time: 48.4 us; the launch traced here: 48.2 us
  Pallas kernels  46.5 us (96%)
  other arithmetic  1.03 us (2%)
  between operations  0.69 us (1%)
    pallas_call x1, Pallas kernels, shards(): pl.pallas_call(functools.partial(kernel, sections, mem), out_shape=(block...  46.5 us
    broadcast_in_dim x1, other arithmetic, shards(): jnp.where(token_row & (section_now == sections - 1), edge, returned)[None]  1.02 us

profile of v5, /device:TPU:5, one launch (start us, length us, event | category | flops | bytes accessed | tf_op | source)
XLA Modules:
  0.0 48.2 jit_solution(15114100729606863695)
XLA Ops:
  0.7 0.0 copy-start
  0.7 0.0 copy-start.1
  0.7 46.5 %shard_map.104 = (bf16[144,1024]{1,0:T(8,128)(2,1)S(1)}, bf16[144,1024]{1,0:T(8,128)(2,1)S(1)}) custom-call(bf16[144,1024]{1,0:T(8,128)(2,1)} %bitcast.13, bf16[144,1024]{1,0:T(8,128)(2,1)} %bitcast.14, bf16[144,1024]{1,0:T(8,128)(2,1)} %bitcast.15, bf16[1,1024]{1,0:T(2,128)(2,1)} %gain_h.1, bf16[1024,1024]{1,0:T(8,128)(2,1)} %bitcast.10, ...), custom_call_target="tpu_custom_call" | custom-call | tf_op jit(solution)/shard_map/pallas_call | solution.py:654
  47.2 0.0 copy-done
  47.2 0.0 copy-done.1
  47.2 1.0 %select_bitcast_fusion = (bf16[1,144,1024]{2,1,0:T(8,128)(2,1)}, bf16[1,144,1024]{2,1,0:T(8,128)(2,1)}) fusion(bf16[144,1024]{1,0:T(8,128)(2,1)S(1)} %get-tuple-element.5, bf16[128,1024]{1,0:T(8,128)(2,1)S(1)} %copy-done, pred[144]{0:T(512)(128)(4,1)S(1)} %fusion, bf16[144,1024]{1,0:T(8,128)(2,1)S(1)} %get-tuple-element.4, bf16[128,1024]{1,0:T(8,128)(2,1)S(1)} %copy-done.1, ...), kind=kLoop, calls=%fused_computation | loop fusion | flops 294912 | bytes 1704224 | tf_op jit(solution)/shard_map/broadcast_in_dim | solution.py:697
  (2 shorter events, 0.0 us)
Async XLA Ops:
  0.7 46.5 %copy-start = (bf16[128,1024]{1,0:T(8,128)(2,1)S(1)}, bf16[128,1024]{1,0:T(8,128)(2,1)}, u32[]{:S(2)}) copy-start(bf16[128,1024]{1,0:T(8,128)(2,1)} %param.13) | copy-start | bytes 786436
  0.7 46.5 %copy-start.1 = (bf16[128,1024]{1,0:T(8,128)(2,1)S(1)}, bf16[128,1024]{1,0:T(8,128)(2,1)}, u32[]{:S(2)}) copy-start(bf16[128,1024]{1,0:T(8,128)(2,1)} %param.12) | copy-start | bytes 786436

commit v6 on v5

--- a/solution.py
+++ b/solution.py
@@ -16,8 +16,8 @@
 LOCAL = KV_HEADS // PAIR
 SHARED = HEADS // KV_HEADS
 LANES = 128
-PIECES = 4
-SPLIT = 2
+PIECES = 2
+SPLIT = 4
 FOLD = 8
 UNROLL = 3
 
@@ -483,17 +483,17 @@
         def copy(index, one):
             return remote(
                 src.at[one], dst.at[one],
-                sec_send.at[at, index], sec_recv.at[at, index], {"section": where},
+                sec_send.at[index], sec_recv.at[index], {"section": where},
             )
 
-        small = copy(0, pl.ds(begin, mem - begin)) if begin < mem else None
-        large = copy(1, place)
+        small = copy(2 * rounds + at // rounds, pl.ds(begin, mem - begin)) if begin < mem else None
+        large = copy(at, place)
         around = remote(
-            src.at[place], via.at[place], sec_send.at[at, 1], via_recv.at[at], {"section": edge}
+            src.at[place], via.at[place], sec_send.at[at], via_recv.at[at], {"section": edge}
         )
         onward = remote(
             via.at[place], dst.at[place],
-            sec_send.at[at, 1], sec_recv.at[at, 1], {"section": target},
+            sec_send.at[at], sec_recv.at[at], {"section": target},
         )
         if detour:
             turns = jnp.logical_and(section == turning, core == 1)
@@ -679,7 +679,7 @@
             dma((7,)), dma((3,)), dma((4 + rounds,)),
             dma((2, LOCAL)), dma((2, LOCAL, 2)),
             dma((LOCAL,)), dma((LOCAL,)),
-            dma((2 * rounds, 2)), dma((2 * rounds, 2)),
+            dma((2 * rounds + 2,)), dma((2 * rounds + 2,)),
             dma((3, LOCAL)), dma((3, LOCAL)),
             dma((2 * rounds,)),
         ],

time: 48.4 us -> 48.3 us (level)
  no operation moved by 1% of the time
where the time goes in v6:
time: 48.3 us; the launch traced here: 48.2 us
  Pallas kernels  46.4 us (96%)
  other arithmetic  1.03 us (2%)
  between operations  0.69 us (1%)
    pallas_call x1, Pallas kernels, shards(): pl.pallas_call(functools.partial(kernel, sections, mem), out_shape=(block...  46.4 us
    broadcast_in_dim x1, other arithmetic, shards(): jnp.where(token_row & (section_now == sections - 1), edge, returned)[None]  1.02 us

profile of v6, /device:TPU:5, one launch (start us, length us, event | category | flops | bytes accessed | tf_op | source)
XLA Modules:
  0.0 48.2 jit_solution(5113565578309561797)
XLA Ops:
  0.7 0.0 copy-start
  0.7 0.0 copy-start.1
  0.7 46.4 %shard_map.104 = (bf16[144,1024]{1,0:T(8,128)(2,1)S(1)}, bf16[144,1024]{1,0:T(8,128)(2,1)S(1)}) custom-call(bf16[144,1024]{1,0:T(8,128)(2,1)} %bitcast.13, bf16[144,1024]{1,0:T(8,128)(2,1)} %bitcast.14, bf16[144,1024]{1,0:T(8,128)(2,1)} %bitcast.15, bf16[1,1024]{1,0:T(2,128)(2,1)} %gain_h.1, bf16[1024,1024]{1,0:T(8,128)(2,1)} %bitcast.10, ...), custom_call_target="tpu_custom_call" | custom-call | tf_op jit(solution)/shard_map/pallas_call | solution.py:654
  47.1 0.0 copy-done
  47.1 0.0 copy-done.1
  47.1 1.0 %select_bitcast_fusion = (bf16[1,144,1024]{2,1,0:T(8,128)(2,1)}, bf16[1,144,1024]{2,1,0:T(8,128)(2,1)}) fusion(bf16[144,1024]{1,0:T(8,128)(2,1)S(1)} %get-tuple-element.5, bf16[128,1024]{1,0:T(8,128)(2,1)S(1)} %copy-done, pred[144]{0:T(512)(128)(4,1)S(1)} %fusion, bf16[144,1024]{1,0:T(8,128)(2,1)S(1)} %get-tuple-element.4, bf16[128,1024]{1,0:T(8,128)(2,1)S(1)} %copy-done.1, ...), kind=kLoop, calls=%fused_computation | loop fusion | flops 294912 | bytes 1704224 | tf_op jit(solution)/shard_map/broadcast_in_dim | solution.py:697
  (2 shorter events, 0.0 us)
Async XLA Ops:
  0.7 46.5 %copy-start = (bf16[128,1024]{1,0:T(8,128)(2,1)S(1)}, bf16[128,1024]{1,0:T(8,128)(2,1)}, u32[]{:S(2)}) copy-start(bf16[128,1024]{1,0:T(8,128)(2,1)} %param.13) | copy-start | bytes 786436
  0.7 46.5 %copy-start.1 = (bf16[128,1024]{1,0:T(8,128)(2,1)S(1)}, bf16[128,1024]{1,0:T(8,128)(2,1)}, u32[]{:S(2)}) copy-start(bf16[128,1024]{1,0:T(8,128)(2,1)} %param.12) | copy-start | bytes 786436
